TPU v7x, 256 devices: a whole 4x4x8 slice. The times are simulated.
256 devices in a mesh: depth: 2 (over core), tile: 128 (over z, y, x).
Axes of the slice: x: 4, y: 4, z: 8, core: 2. Of those that a mesh axis runs over, the one named last changes fastest.
Arguments:
- transmission: float32 [2, 4, 8192, 2048], P(None, 'depth', 'tile'), may hold values from -1 to 1, as said below
- probe: float32 [2, 128, 128], replicated, may hold values from -4 to 4
- scan_rows: int32 [1024], P('tile'), may hold values from 0 to 8064, as said below
- scan_cols: int32 [1024], P('tile'), may hold values from 0 to 1920
- tile_counts: int32 [128], replicated, may hold values from 1 to 8, as said below
- diffraction: float32 [1024, 128, 128], P('tile'), may hold values from 0 to 2
Outputs:
- object_grad: float32 [2, 4, 8192, 2048], P(None, 'depth', 'tile')
- probe_grad: float32 [2, 128, 128], P(None, 'depth')
Inputs may be any that keep to these rules, and one draw needn't show every extreme that they name: `scan_rows`: slot i's row lies within [t * 64 - 128/2, t * 64 + 64 - 128/2) for t = i // 8, clipped to the specimen; both ends of the specimen are reached. `tile_counts`: some strip has all 8 slots filled and some strip only one. `transmission`: every entry has magnitude between 0.8 and 1.
All inputs are finite; a program needn't handle non-finite values.
Results may differ from a plain program's by a relative error of at most 0.0003.
Values sent between devices are 32-bit elements; how exact they have to be, the bound alone decides.
No kernel may reach another device: no remote copies, remote signals or barrier semaphores. Data moves between devices by JAX's collectives and lax.ppermute only.
A program may use at most 320 MiB of HBM per device.

v0:
```python
import functools
import math

import jax
import jax.numpy as jnp
import numpy as np
from jax import lax
from jax.experimental import pallas as pl
from jax.experimental.pallas import tpu as pltpu
from jax.sharding import PartitionSpec as P


FRESNEL = 0.5
AXES = ("depth", "tile")
F32 = jnp.float32
BF16 = jnp.bfloat16
RANK = {1: 0, 2: 1, 4: 2, 8: 3, 16: 4, 32: 5, 64: 6}
VMEM = pl.BlockSpec(memory_space=pltpu.VMEM)
SMEM = pl.BlockSpec(memory_space=pltpu.SMEM)


@functools.lru_cache(None)
def tables(size):
    index = np.arange(size)
    angle = 2.0 * math.pi / size * ((index[:, None] * index[None, :]) % size)
    cosine = np.cos(angle) / math.sqrt(size)
    sine = np.sin(angle) / math.sqrt(size)
    freq = ((index + size // 2) % size - size // 2).astype(np.float64)
    phase = FRESNEL * math.pi / size * (freq[:, None] ** 2 + freq[None, :] ** 2)

    def halves(matrix):
        high = matrix.astype(BF16)
        low = (matrix - high.astype(np.float64)).astype(BF16)
        return high, low

    fwd = np.block([[cosine, -sine], [sine, cosine]])
    inv = np.block([[cosine, sine], [-sine, cosine]])
    kern = np.stack([np.cos(phase), np.sin(phase)]).astype(np.float32)
    return np.stack([*halves(fwd), *halves(inv)]), kern


def window_of(col, cols, size):
    block = jnp.minimum(col // size, cols // size - 2)
    return pl.multiple_of(block * size, size), col - block * size


def cut_piece(trans_ref, out_ref, item, col):
    parts, group, _, cols = trans_ref.shape
    size = out_ref.shape[-1]
    base, shift = window_of(col, cols, size)
    for part in range(parts):
        for s in range(group):
            wide = trans_ref[part, s, :, pl.ds(base, 2 * size)]
            turned = pltpu.roll(wide, lax.rem(2 * size - shift, 2 * size), 1)
            out_ref[item, part, s] = turned[:, :size]


def cut_own_kernel(cols_ref, trans_ref, same_ref, other_ref):
    depth = lax.axis_index("depth")

    @pl.loop(0, same_ref.shape[0])
    def _(item):
        cut_piece(trans_ref, same_ref, item, cols_ref[2 * item + depth])
        cut_piece(trans_ref, other_ref, item, cols_ref[2 * item + 1 - depth])


def cut_halo_kernel(up_cols_ref, dn_cols_ref, trans_ref, up_same, up_other, dn_same, dn_other):
    depth = lax.axis_index("depth")

    @pl.loop(0, up_same.shape[0])
    def _(item):
        same = 2 * item + depth
        other = 2 * item + 1 - depth
        cut_piece(trans_ref, up_same, item, up_cols_ref[same])
        cut_piece(trans_ref, up_other, item, up_cols_ref[other])
        cut_piece(trans_ref, dn_same, item, dn_cols_ref[same])
        cut_piece(trans_ref, dn_other, item, dn_cols_ref[other])


def split3(x):
    high = x.astype(BF16)
    low = (x - high.astype(F32)).astype(BF16)
    return high, low


def right_mul(x, dft_ref, which):
    high, low = split3(x)
    table = jnp.concatenate([dft_ref[which], dft_ref[which], dft_ref[which + 1]], axis=0)
    return jnp.dot(jnp.concatenate([high, low, high], axis=1), table, preferred_element_type=F32)


def left_mul(dft_ref, which, x):
    high, low = split3(x)
    table = jnp.concatenate([dft_ref[which], dft_ref[which + 1], dft_ref[which]], axis=1)
    return jnp.dot(table, jnp.concatenate([high, high, low], axis=0), preferred_element_type=F32)


def swap(x):
    half = x.shape[0] // 2
    top = jnp.concatenate([x[:half, :half], x[half:, :half]], axis=1)
    bottom = jnp.concatenate([x[:half, half:], x[half:, half:]], axis=1)
    return jnp.concatenate([top, bottom], axis=0)


def compute_kernel(
    counts_ref,
    rows_ref,
    own_same,
    own_other,
    up_same,
    up_other,
    dn_same,
    dn_other,
    probe_ref,
    diff_ref,
    dft_ref,
    kern_ref,
    g_own_same,
    g_own_other,
    g_up_same,
    g_up_other,
    g_dn_same,
    g_dn_other,
    p_same,
    p_other,
    stack,
    grads,
    trans,
    waves,
    back,
    probe_sum,
):
    depth, tile = lax.axis_index("depth"), lax.axis_index("tile")
    filled = counts_ref[tile]
    items, parts, per, strip, size = own_same.shape
    pairs = range(items // 2)
    slices = 2 * per
    half = size // 2
    mine, theirs = depth * per, (1 - depth) * per
    slots = [2 * item + depth for item in range(items)]
    outs = (
        (g_up_same, g_up_other, 0, half),
        (g_own_same, g_own_other, half, strip),
        (g_dn_same, g_dn_other, half + strip, half),
    )
    live = [(slot < filled).astype(F32) for slot in slots]
    kc = jnp.concatenate([kern_ref[0], kern_ref[0]], axis=0)
    ks = jnp.concatenate([kern_ref[1], kern_ref[1]], axis=0)

    for item in range(items):
        offset = rows_ref[slots[item]] - (tile * strip - half)
        p, q = item // 2, item % 2
        for part in range(parts):
            for s in range(per):
                for base, same, other, at, length in (
                    (0, up_same, up_other, strip - half, half),
                    (half, own_same, own_other, 0, strip),
                    (half + strip, dn_same, dn_other, 0, half),
                ):
                    stack[mine + s, pl.ds(base, length), :] = same[item, part, s, at : at + length]
                    stack[theirs + s, pl.ds(base, length), :] = other[item, part, s, at : at + length]
            for s in range(slices):
                trans[p, s, part * size : (part + 1) * size, q * size : (q + 1) * size] = stack[
                    s, pl.ds(offset, size), :
                ]
            waves[p, 0, part * size : (part + 1) * size, q * size : (q + 1) * size] = probe_ref[part] * live[item]

    def chain(xs, middle):
        xs = [swap(left_mul(dft_ref, 2, x)) for x in xs]
        xs = [middle(p, right_mul(x, dft_ref, 0)) for p, x in enumerate(xs)]
        xs = [swap(right_mul(x, dft_ref, 2)) for x in xs]
        return [left_mul(dft_ref, 0, x) for x in xs]

    def kernel_times(sign):
        def middle(p, x):
            re, im = x[:, :size], x[:, size:]
            if sign > 0:
                return jnp.concatenate([re * kc - im * ks, im * kc + re * ks], axis=1)
            return jnp.concatenate([re * kc + im * ks, im * kc - re * ks], axis=1)

        return middle

    def residual(p, x):
        re, im = x[:, :size], x[:, size:]
        measured = jnp.concatenate([diff_ref[slots[2 * p]], diff_ref[slots[2 * p + 1]]], axis=0)
        gap = re * re + im * im - measured
        return jnp.concatenate([gap * re, gap * im], axis=1)

    def forward_times(p, s):
        t_re, t_im = trans[p, s, :size], trans[p, s, size:]
        w_re, w_im = waves[p, s, :size], waves[p, s, size:]
        return jnp.concatenate([t_re * w_re - t_im * w_im, t_re * w_im + t_im * w_re], axis=0)

    def adjoint_times(s, alongs):
        for p, along in enumerate(alongs):
            a_re, a_im = along[:size], along[size:]
            w_re, w_im = waves[p, s, :size], waves[p, s, size:]
            waves[p, s, :size] = w_re * a_re + w_im * a_im
            waves[p, s, size:] = w_re * a_im - w_im * a_re
            t_re, t_im = trans[p, s, :size], trans[p, s, size:]
            back[p, :size] = t_re * a_re + t_im * a_im
            back[p, size:] = t_re * a_im - t_im * a_re

    @pl.loop(0, slices - 1)
    def _forward(s):
        for p, x in enumerate(chain([forward_times(p, s) for p in pairs], kernel_times(-1))):
            waves[p, s + 1] = x

    adjoint_times(slices - 1, chain([forward_times(p, slices - 1) for p in pairs], residual))

    @pl.loop(0, slices - 1)
    def _backward(i):
        adjoint_times(slices - 2 - i, chain([back[p] for p in pairs], kernel_times(1)))

    for part in range(parts):
        rows = slice(part * size, (part + 1) * size)
        total = back[0, rows, :size] + back[0, rows, size:]
        for p in pairs[1:]:
            total = total + back[p, rows, :size] + back[p, rows, size:]
        probe_sum[...] = total
        p_same[part] = probe_sum[pl.ds(depth * half, half)]
        p_other[part] = probe_sum[pl.ds((1 - depth) * half, half)]

    for item in range(items):
        offset = rows_ref[slots[item]] - (tile * strip - half)
        p, q = item // 2, item % 2
        for part in range(parts):
            grads[...] = jnp.zeros_like(grads)
            for s in range(slices):
                grads[s, pl.ds(offset, size), :] = waves[
                    p, s, part * size : (part + 1) * size, q * size : (q + 1) * size
                ]
            for s in range(per):
                for same, other, base, length in outs:
                    same[item, part, s] = grads[mine + s, base : base + length]
                    other[item, part, s] = grads[theirs + s, base : base + length]


def add_blocks(out_ref, cols_ref, filled, block_ref, parity):
    count, parts, per, _, size = block_ref.shape
    cols = out_ref.shape[-1]

    @pl.loop(0, count)
    def _(item):
        slot = 2 * item + parity

        @pl.when(slot < filled)
        def _():
            base, shift = window_of(cols_ref[slot], cols, size)
            for part in range(parts):
                for s in range(per):
                    block = block_ref[item, part, s]
                    wide = jnp.concatenate([block, jnp.zeros_like(block)], axis=1)
                    out_ref[part, s, :, pl.ds(base, 2 * size)] += pltpu.roll(wide, shift, 1)


def place_own_kernel(counts_ref, own_cols, own_same, own_other, out_ref):
    depth, tile = lax.axis_index("depth"), lax.axis_index("tile")
    out_ref[...] = jnp.zeros_like(out_ref)
    add_blocks(out_ref, own_cols, counts_ref[tile], own_same, depth)
    add_blocks(out_ref, own_cols, counts_ref[tile], own_other, 1 - depth)


def place_halo_kernel(
    counts_ref, up_cols, dn_cols, up_same, up_other, dn_same, dn_other, so_far, out_ref
):
    depth, tile = lax.axis_index("depth"), lax.axis_index("tile")
    last = counts_ref.shape[0] - 1
    above = jnp.where(tile > 0, counts_ref[jnp.maximum(tile - 1, 0)], 0)
    below = jnp.where(tile < last, counts_ref[jnp.minimum(tile + 1, last)], 0)
    out_ref[...] = so_far[...]
    add_blocks(out_ref, up_cols, above, up_same, depth)
    add_blocks(out_ref, up_cols, above, up_other, 1 - depth)
    add_blocks(out_ref, dn_cols, below, dn_same, depth)
    add_blocks(out_ref, dn_cols, below, dn_other, 1 - depth)


def call(kernel, in_specs, out_shapes, args, scratch=(), cost=(1 << 20, 1 << 20), aliases=None, limit=16):
    single = not isinstance(out_shapes, (list, tuple))
    return pl.pallas_call(
        kernel,
        out_shape=out_shapes if single else tuple(out_shapes),
        in_specs=in_specs,
        out_specs=VMEM if single else tuple(VMEM for _ in out_shapes),
        scratch_shapes=list(scratch),
        input_output_aliases=aliases or {},
        cost_estimate=pl.CostEstimate(flops=cost[0], bytes_accessed=cost[1], transcendentals=0),
        compiler_params=pltpu.CompilerParams(vmem_limit_bytes=limit << 20),
    )(*args)


def work(transmission, probe, scan_rows, scan_cols, tile_counts, diffraction):
    parts, per, strip, _ = transmission.shape
    size = probe.shape[-1]
    half = size // 2
    slots = scan_rows.shape[0]
    n_depth, n_tile = lax.axis_size("depth"), lax.axis_size("tile")
    slices = n_depth * per
    items = slots // n_depth

    def send(value, cross, by):
        pairs = [
            (d * n_tile + t, (d + cross) % n_depth * n_tile + t + by)
            for d in range(n_depth)
            for t in range(n_tile)
            if 0 <= t + by < n_tile
        ]
        return lax.ppermute(value, AXES, pairs)

    up_cols = send(scan_cols, 0, 1)
    dn_cols = send(scan_cols, 0, -1)
    bank = jax.ShapeDtypeStruct((items, parts, per, strip, size), F32)
    own_same, own_cross = call(
        cut_own_kernel, [SMEM, VMEM], [bank, bank], (scan_cols, transmission)
    )
    own_other = send(own_cross, 1, 0)
    up_s, up_x, dn_s, dn_x = call(
        cut_halo_kernel, [SMEM, SMEM, VMEM], [bank] * 4, (up_cols, dn_cols, transmission)
    )
    halos = (send(dn_s, 0, 1), send(dn_x, 1, 1), send(up_s, 0, -1), send(up_x, 1, -1))

    results = call(
        compute_kernel,
        [SMEM, SMEM] + [VMEM] * 10,
        [bank] * 6 + [jax.ShapeDtypeStruct((parts, half, size), F32)] * 2,
        (tile_counts, scan_rows, own_same, own_other, *halos, probe, diffraction)
        + tuple(jnp.asarray(v) for v in tables(size)),
        scratch=[
            pltpu.VMEM((slices, 2 * half + strip, size), F32),
            pltpu.VMEM((slices, 2 * half + strip, size), F32),
            pltpu.VMEM((items // 2, slices, 2 * size, 2 * size), F32),
            pltpu.VMEM((items // 2, slices, 2 * size, 2 * size), F32),
            pltpu.VMEM((items // 2, 2 * size, 2 * size), F32),
            pltpu.VMEM((size, size), F32),
        ],
        cost=(6 << 30, 8 << 20),
        limit=24,
    )
    g_own_s, g_own_x, g_up_s, g_up_x, g_dn_s, g_dn_x, p_same, p_other = results

    total = p_same + send(p_other, 1, 0)
    own_back = send(g_own_x, 1, 0)
    steps = [1 << k for k in range(n_tile.bit_length() - 1)]
    order = sorted(steps, key=lambda step: RANK.get(step, 0))
    for step in order:
        pairs = [(d * n_tile + t, d * n_tile + (t ^ step)) for d in range(n_depth) for t in range(n_tile)]
        total = total + lax.ppermute(total, AXES, pairs)
    up_same = send(g_dn_s, 0, 1)
    up_other = send(g_dn_x, 1, 1)
    dn_same = send(g_up_s, 0, -1)
    dn_other = send(g_up_x, 1, -1)

    grad_shape = jax.ShapeDtypeStruct(transmission.shape, F32)
    grad = call(
        place_own_kernel,
        [SMEM] * 2 + [VMEM] * 2,
        grad_shape,
        (tile_counts, scan_cols, g_own_s, own_back),
    )
    grad = call(
        place_halo_kernel,
        [SMEM] * 3 + [VMEM] * 5,
        grad_shape,
        (tile_counts, up_cols, dn_cols, up_same, up_other, dn_same, dn_other, grad),
    )
    return (grad, total)


def solution(mesh):
    placed = (P(None, "depth", "tile", None), P(), P("tile"), P("tile"), P(), P("tile", None, None))
    return jax.shard_map(
        work,
        mesh=mesh,
        in_specs=placed,
        out_specs=(P(None, "depth", "tile", None), P(None, "depth", None)),
        check_vma=False,
    )
```

profile of v0, /device:TPU:63, one launch (start us, length us, event | category | flops | bytes accessed | tf_op | source)
XLA Modules:
  0.0 142.5 jit_solution(1988750139388623965)
XLA Ops:
  0.6 2.5 %collective-permute-start.1 = (s32[8]{0:T(128)}, s32[8]{0:T(128)S(1)}, u32[]{:S(2)}, u32[]{:S(2)}) collective-permute-start(s32[8]{0:T(128)} %own_cols.1), channel_id=1, source_target_pairs={{1,0},{2,1},{3,2},{4,3},{5,4},{6,5},{7,6},{8,7},{9,8},{10,9},{11,1... | collective-permute-start | bytes 104 | tf_op jit(solution)/shard_map/ppermute | solution.py:308
  3.1 7.0 %collective-permute-start = (s32[8]{0:T(128)}, s32[8]{0:T(128)S(1)}, u32[]{:S(2)}, u32[]{:S(2)}) collective-permute-start(s32[8]{0:T(128)} %own_cols.1), channel_id=1, source_target_pairs={{0,1},{1,2},{2,3},{3,4},{4,5},{5,6},{6,7},{7,8},{8,9},{9,10},{10,1... | collective-permute-start | bytes 104 | tf_op jit(solution)/shard_map/ppermute | solution.py:308
  10.2 1.6 %copy-done = f32[2,2,64,2048]{3,2,1,0:T(8,128)S(1)} copy-done((f32[2,2,64,2048]{3,2,1,0:T(8,128)S(1)}, f32[2,2,64,2048]{3,2,1,0:T(8,128)}, u32[]{:S(2)}) %copy-start) | copy-done | bytes 2097176
  11.7 0.7 copy-done.2
  12.4 0.0 copy-start.8
  12.4 0.0 copy-start.9
  12.4 1.4 shard_map.95
  13.9 1.3 collective-permute-start.2
  15.2 0.0 collective-permute-done.1.dn_cols_ref.dn_cols
  15.2 0.0 collective-permute-done.up_cols_ref.up_cols
  15.2 1.9 %shard_map.96 = (f32[4,2,2,64,128]{4,3,2,1,0:T(8,128)S(1)}, f32[4,2,2,64,128]{4,3,2,1,0:T(8,128)S(1)}, f32[4,2,2,64,128]{4,3,2,1,0:T(8,128)S(1)}, f32[4,2,2,64,128]{4,3,2,1,0:T(8,128)S(1)}) custom-call(s32[8]{0:T(128)S(1)} %collective-permute-done.up_cols_ref.up_cols, s32[8]{0:T(128)S(1)} %collective-permute-done.1.dn_cols_ref.dn_cols, ...), custom_call_target="tpu_custom_call" | custom-call | flops 1048576 | bytes 1048576 | tf_op jit(solution)/shard_map/pallas_call | solution.py:280
  17.2 3.6 %collective-permute-start.3 = (f32[4,2,2,64,128]{4,3,2,1,0:T(8,128)S(1)}, f32[4,2,2,64,128]{4,3,2,1,0:T(8,128)S(1)}, u32[]{:S(2)}, u32[]{:S(2)}) collective-permute-start(f32[4,2,2,64,128]{4,3,2,1,0:T(8,128)S(1)} %get-tuple-element.18), channel_id=1, source_target_pairs={{0,1},{1,2},{2,3},{3,4},{4,5},{5,6},{6,7},{7,8},{8,9},{9,10},{10,1... | collective-permute-start | bytes 1572872 | tf_op jit(solution)/shard_map/ppermute | solution.py:308
  20.8 3.9 %collective-permute-start.4 = (f32[4,2,2,64,128]{4,3,2,1,0:T(8,128)S(1)}, f32[4,2,2,64,128]{4,3,2,1,0:T(8,128)S(1)}, u32[]{:S(2)}, u32[]{:S(2)}) collective-permute-start(f32[4,2,2,64,128]{4,3,2,1,0:T(8,128)S(1)} %get-tuple-element.19), channel_id=1, source_target_pairs={{0,129},{1,130},{2,131},{3,132},{4,133},{5,134},{6,135},{7,136},{8... | collective-permute-start | bytes 1572872 | tf_op jit(solution)/shard_map/ppermute | solution.py:308
  24.7 3.6 %collective-permute-start.5 = (f32[4,2,2,64,128]{4,3,2,1,0:T(8,128)S(1)}, f32[4,2,2,64,128]{4,3,2,1,0:T(8,128)S(1)}, u32[]{:S(2)}, u32[]{:S(2)}) collective-permute-start(f32[4,2,2,64,128]{4,3,2,1,0:T(8,128)S(1)} %get-tuple-element.20), channel_id=1, source_target_pairs={{1,0},{2,1},{3,2},{4,3},{5,4},{6,5},{7,6},{8,7},{9,8},{10,9},{11,1... | collective-permute-start | bytes 1572872 | tf_op jit(solution)/shard_map/ppermute | solution.py:308
  28.3 1.9 %collective-permute-start.6 = (f32[4,2,2,64,128]{4,3,2,1,0:T(8,128)S(1)}, f32[4,2,2,64,128]{4,3,2,1,0:T(8,128)S(1)}, u32[]{:S(2)}, u32[]{:S(2)}) collective-permute-start(f32[4,2,2,64,128]{4,3,2,1,0:T(8,128)S(1)} %get-tuple-element.21), channel_id=1, source_target_pairs={{1,128},{2,129},{3,130},{4,131},{5,132},{6,133},{7,134},{8,135},{9... | collective-permute-start | bytes 1572872 | tf_op jit(solution)/shard_map/ppermute | solution.py:308
  30.3 0.0 collective-permute-done.2.own_other
  30.3 2.2 %collective-permute-done.3.up_same = f32[4,2,2,64,128]{4,3,2,1,0:T(8,128)S(1)} collective-permute-done((f32[4,2,2,64,128]{4,3,2,1,0:T(8,128)S(1)}, f32[4,2,2,64,128]{4,3,2,1,0:T(8,128)S(1)}, u32[]{:S(2)}, u32[]{:S(2)}) %collective-permute-start.3) | collective-permute-done | bytes 524320 | tf_op jit(solution)/shard_map/ppermute | solution.py:308
  32.5 11.7 %collective-permute-done.4.up_other = f32[4,2,2,64,128]{4,3,2,1,0:T(8,128)S(1)} collective-permute-done((f32[4,2,2,64,128]{4,3,2,1,0:T(8,128)S(1)}, f32[4,2,2,64,128]{4,3,2,1,0:T(8,128)S(1)}, u32[]{:S(2)}, u32[]{:S(2)}) %collective-permute-start.4) | collective-permute-done | bytes 524320 | tf_op jit(solution)/shard_map/ppermute | solution.py:308
  44.2 11.5 %collective-permute-done.6.dn_other = f32[4,2,2,64,128]{4,3,2,1,0:T(8,128)S(1)} collective-permute-done((f32[4,2,2,64,128]{4,3,2,1,0:T(8,128)S(1)}, f32[4,2,2,64,128]{4,3,2,1,0:T(8,128)S(1)}, u32[]{:S(2)}, u32[]{:S(2)}) %collective-permute-start.6) | collective-permute-done | bytes 524320 | tf_op jit(solution)/shard_map/ppermute | solution.py:308
  55.7 0.0 copy-start.3
  55.7 11.9 %shard_map.97 = (f32[4,2,2,64,128]{4,3,2,1,0:T(8,128)S(1)}, f32[4,2,2,64,128]{4,3,2,1,0:T(8,128)S(1)}, f32[4,2,2,64,128]{4,3,2,1,0:T(8,128)S(1)}, f32[4,2,2,64,1...) custom-call(s32[128]{0:T(128)S(1)} %copy-done.4, ...), custom_call_target="tpu_custom_call" | custom-call | flops 6442450944 | bytes 8388608 | tf_op jit(solution)/shard_map/pallas_call | solution.py:280
  67.7 0.1 collective-permute-start.12
  67.8 1.2 collective-permute-done.12
  69.0 0.1 collective-permute-start.13
  69.1 3.5 %collective-permute-done.13 = f32[2,64,128]{2,1,0:T(8,128)S(1)} collective-permute-done((f32[2,64,128]{2,1,0:T(8,128)S(1)}, f32[2,64,128]{2,1,0:T(8,128)S(1)}, u32[]{:S(2)}, u32[]{:S(2)}) %collective-permute-start.13) | collective-permute-done | bytes 65568 | tf_op jit(solution)/shard_map/ppermute | solution.py:347
  72.6 0.1 collective-permute-start.14
  72.7 4.6 %collective-permute-done.14 = f32[2,64,128]{2,1,0:T(8,128)S(1)} collective-permute-done((f32[2,64,128]{2,1,0:T(8,128)S(1)}, f32[2,64,128]{2,1,0:T(8,128)S(1)}, u32[]{:S(2)}, u32[]{:S(2)}) %collective-permute-start.14) | collective-permute-done | bytes 65568 | tf_op jit(solution)/shard_map/ppermute | solution.py:347
  77.3 0.1 collective-permute-start.15
  77.4 3.1 %collective-permute-done.15 = f32[2,64,128]{2,1,0:T(8,128)S(1)} collective-permute-done((f32[2,64,128]{2,1,0:T(8,128)S(1)}, f32[2,64,128]{2,1,0:T(8,128)S(1)}, u32[]{:S(2)}, u32[]{:S(2)}) %collective-permute-start.15) | collective-permute-done | bytes 65568 | tf_op jit(solution)/shard_map/ppermute | solution.py:347
  80.5 0.1 collective-permute-start.16
  80.6 4.6 %collective-permute-done.16 = f32[2,64,128]{2,1,0:T(8,128)S(1)} collective-permute-done((f32[2,64,128]{2,1,0:T(8,128)S(1)}, f32[2,64,128]{2,1,0:T(8,128)S(1)}, u32[]{:S(2)}, u32[]{:S(2)}) %collective-permute-start.16) | collective-permute-done | bytes 65568 | tf_op jit(solution)/shard_map/ppermute | solution.py:347
  85.3 0.1 collective-permute-start.17
  85.4 3.4 %collective-permute-done.17 = f32[2,64,128]{2,1,0:T(8,128)S(1)} collective-permute-done((f32[2,64,128]{2,1,0:T(8,128)S(1)}, f32[2,64,128]{2,1,0:T(8,128)S(1)}, u32[]{:S(2)}, u32[]{:S(2)}) %collective-permute-start.17) | collective-permute-done | bytes 65568 | tf_op jit(solution)/shard_map/ppermute | solution.py:347
  88.8 6.7 %collective-permute-start.18 = (f32[2,64,128]{2,1,0:T(8,128)S(1)}, f32[2,64,128]{2,1,0:T(8,128)S(1)}, u32[]{:S(2)}, u32[]{:S(2)}) collective-permute-start(f32[2,64,128]{2,1,0:T(8,128)S(1)} %add.29), channel_id=1, source_target_pairs={{0,32},{1,33},{2,34},{3,35},{4,36},{5,37},{6,38},{7,39},{8,40},{9,... | collective-permute-start | bytes 196616 | tf_op jit(solution)/shard_map/ppermute | solution.py:347
  95.5 5.9 %collective-permute-start.11 = (f32[4,2,2,64,128]{4,3,2,1,0:T(8,128)S(1)}, f32[4,2,2,64,128]{4,3,2,1,0:T(8,128)S(1)}, u32[]{:S(2)}, u32[]{:S(2)}) collective-permute-start(f32[4,2,2,64,128]{4,3,2,1,0:T(8,128)S(1)} %get-tuple-element.27), channel_id=1, source_target_pairs={{0,128},{1,129},{2,130},{3,131},{4,132},{5,133},{6,134},{7,135},{8... | collective-permute-start | bytes 1572872 | tf_op jit(solution)/shard_map/ppermute | solution.py:308
  101.4 1.9 %collective-permute-start.7 = (f32[4,2,2,64,128]{4,3,2,1,0:T(8,128)S(1)}, f32[4,2,2,64,128]{4,3,2,1,0:T(8,128)S(1)}, u32[]{:S(2)}, u32[]{:S(2)}) collective-permute-start(f32[4,2,2,64,128]{4,3,2,1,0:T(8,128)S(1)} %get-tuple-element.22), channel_id=1, source_target_pairs={{0,1},{1,2},{2,3},{3,4},{4,5},{5,6},{6,7},{7,8},{8,9},{9,10},{10,1... | collective-permute-start | bytes 1572872 | tf_op jit(solution)/shard_map/ppermute | solution.py:308
  103.3 1.9 %collective-permute-start.8 = (f32[4,2,2,64,128]{4,3,2,1,0:T(8,128)S(1)}, f32[4,2,2,64,128]{4,3,2,1,0:T(8,128)S(1)}, u32[]{:S(2)}, u32[]{:S(2)}) collective-permute-start(f32[4,2,2,64,128]{4,3,2,1,0:T(8,128)S(1)} %get-tuple-element.23), channel_id=1, source_target_pairs={{0,129},{1,130},{2,131},{3,132},{4,133},{5,134},{6,135},{7,136},{8... | collective-permute-start | bytes 1572872 | tf_op jit(solution)/shard_map/ppermute | solution.py:308
  105.2 3.4 %collective-permute-start.9 = (f32[4,2,2,64,128]{4,3,2,1,0:T(8,128)S(1)}, f32[4,2,2,64,128]{4,3,2,1,0:T(8,128)S(1)}, u32[]{:S(2)}, u32[]{:S(2)}) collective-permute-start(f32[4,2,2,64,128]{4,3,2,1,0:T(8,128)S(1)} %get-tuple-element.24), channel_id=1, source_target_pairs={{1,0},{2,1},{3,2},{4,3},{5,4},{6,5},{7,6},{8,7},{9,8},{10,9},{11,1... | collective-permute-start | bytes 1572872 | tf_op jit(solution)/shard_map/ppermute | solution.py:308
  108.6 3.9 %collective-permute-start.10 = (f32[4,2,2,64,128]{4,3,2,1,0:T(8,128)S(1)}, f32[4,2,2,64,128]{4,3,2,1,0:T(8,128)S(1)}, u32[]{:S(2)}, u32[]{:S(2)}) collective-permute-start(f32[4,2,2,64,128]{4,3,2,1,0:T(8,128)S(1)} %get-tuple-element.25), channel_id=1, source_target_pairs={{1,128},{2,129},{3,130},{4,131},{5,132},{6,133},{7,134},{8,135},{9... | collective-permute-start | bytes 1572872 | tf_op jit(solution)/shard_map/ppermute | solution.py:308
  112.5 0.0 collective-permute-done.11.own_other
  112.6 0.1 collective-permute-start.19
  112.7 1.1 shard_map.98.so_far
  113.8 2.9 %collective-permute-done.7.up_same = f32[4,2,2,64,128]{4,3,2,1,0:T(8,128)S(1)} collective-permute-done((f32[4,2,2,64,128]{4,3,2,1,0:T(8,128)S(1)}, f32[4,2,2,64,128]{4,3,2,1,0:T(8,128)S(1)}, u32[]{:S(2)}, u32[]{:S(2)}) %collective-permute-start.7) | collective-permute-done | bytes 524320 | tf_op jit(solution)/shard_map/ppermute | solution.py:308
  116.7 11.7 %collective-permute-done.8.up_other = f32[4,2,2,64,128]{4,3,2,1,0:T(8,128)S(1)} collective-permute-done((f32[4,2,2,64,128]{4,3,2,1,0:T(8,128)S(1)}, f32[4,2,2,64,128]{4,3,2,1,0:T(8,128)S(1)}, u32[]{:S(2)}, u32[]{:S(2)}) %collective-permute-start.8) | collective-permute-done | bytes 524320 | tf_op jit(solution)/shard_map/ppermute | solution.py:308
  128.4 10.6 %collective-permute-done.10.dn_other = f32[4,2,2,64,128]{4,3,2,1,0:T(8,128)S(1)} collective-permute-done((f32[4,2,2,64,128]{4,3,2,1,0:T(8,128)S(1)}, f32[4,2,2,64,128]{4,3,2,1,0:T(8,128)S(1)}, u32[]{:S(2)}, u32[]{:S(2)}) %collective-permute-start.10) | collective-permute-done | bytes 524320 | tf_op jit(solution)/shard_map/ppermute | solution.py:308
  139.0 2.9 %shard_map.99 = f32[2,2,64,2048]{3,2,1,0:T(8,128)} custom-call(s32[128]{0:T(128)S(1)} %copy-done.4, s32[8]{0:T(128)S(1)} %collective-permute-done.up_cols_ref.up_cols, s32[8]{0:T(128)S(1)} %collective-permute-done.1.dn_cols_ref.dn_cols, f32[4,2,2,64,128]{4,3,2,1,0:T(8,128)S(1)} %collective-permute-done.7.up_same, ...), custom_call_target="tpu_custom_call" | custom-call | flops 1048576 | bytes 1048576 | tf_op jit(solution)/shard_map/pallas_call | solution.py:280
  141.9 0.0 collective-permute-done.19
  141.9 0.6 add.31
  (25 shorter events, 0.1 us)
Async XLA Ops:
  0.6 14.6 %collective-permute-start.1 = (s32[8]{0:T(128)}, s32[8]{0:T(128)S(1)}, u32[]{:S(2)}, u32[]{:S(2)}) collective-permute-start(s32[8]{0:T(128)} %own_cols.1), channel_id=1, source_target_pairs={{1,0},{2,1},{3,2},{4,3},{5,4},{6,5},{7,6},{8,7},{9,8},{10,9},{11,1... | collective-permute-start | bytes 104 | tf_op jit(solution)/shard_map/ppermute | solution.py:308
  3.1 12.1 %collective-permute-start = (s32[8]{0:T(128)}, s32[8]{0:T(128)S(1)}, u32[]{:S(2)}, u32[]{:S(2)}) collective-permute-start(s32[8]{0:T(128)} %own_cols.1), channel_id=1, source_target_pairs={{0,1},{1,2},{2,3},{3,4},{4,5},{5,6},{6,7},{7,8},{8,9},{9,10},{10,1... | collective-permute-start | bytes 104 | tf_op jit(solution)/shard_map/ppermute | solution.py:308
  10.2 1.6 %copy-start = (f32[2,2,64,2048]{3,2,1,0:T(8,128)S(1)}, f32[2,2,64,2048]{3,2,1,0:T(8,128)}, u32[]{:S(2)}) copy-start(f32[2,2,64,2048]{3,2,1,0:T(8,128)} %trans_ref.3) | copy-start | bytes 6291460
  11.7 0.7 copy-start.2
  12.4 2.8 %copy-start.1 = (f32[2,2,64,2048]{3,2,1,0:T(8,128)S(1)}, f32[2,2,64,2048]{3,2,1,0:T(8,128)}, u32[]{:S(2)}) copy-start(f32[2,2,64,2048]{3,2,1,0:T(8,128)} %trans_ref.3) | copy-start | bytes 6291460
  12.4 43.3 %copy-start.4 = (s32[128]{0:T(128)S(1)}, s32[128]{0:T(128)}, u32[]{:S(2)}) copy-start(s32[128]{0:T(128)} %counts_ref.5) | copy-start | bytes 1540
  12.4 43.3 %copy-start.5 = (f32[8,128,128]{2,1,0:T(8,128)S(1)}, f32[8,128,128]{2,1,0:T(8,128)}, u32[]{:S(2)}) copy-start(f32[8,128,128]{2,1,0:T(8,128)} %diff_ref.1) | copy-start | bytes 1572868
  12.4 43.3 %copy-start.6 = (f32[2,128,128]{2,1,0:T(8,128)S(1)}, f32[2,128,128]{2,1,0:T(8,128)}, u32[]{:S(2)}) copy-start(f32[2,128,128]{2,1,0:T(8,128)} %probe_ref.1) | copy-start | bytes 393220
  12.4 43.3 %copy-start.7 = (s32[8]{0:T(128)S(1)}, s32[8]{0:T(128)}, u32[]{:S(2)}) copy-start(s32[8]{0:T(128)} %rows_ref.1) | copy-start | bytes 100
  12.4 43.3 %copy-start.8 = (bf16[4,256,256]{2,1,0:T(8,128)(2,1)S(1)}, bf16[4,256,256]{2,1,0:T(8,128)(2,1)}, u32[]{:S(2)}) copy-start(bf16[4,256,256]{2,1,0:T(8,128)(2,1)} %constant.4.clone.dft_ref) | copy-start | bytes 1572868
  12.4 43.3 %copy-start.9 = (f32[2,128,128]{2,1,0:T(8,128)S(1)}, f32[2,128,128]{2,1,0:T(8,128)}, u32[]{:S(2)}) copy-start(f32[2,128,128]{2,1,0:T(8,128)} %constant.5.clone.kern_ref) | copy-start | bytes 393220
  13.9 16.4 %collective-permute-start.2 = (f32[4,2,2,64,128]{4,3,2,1,0:T(8,128)S(1)}, f32[4,2,2,64,128]{4,3,2,1,0:T(8,128)S(1)}, u32[]{:S(2)}, u32[]{:S(2)}) collective-permute-start(f32[4,2,2,64,128]{4,3,2,1,0:T(8,128)S(1)} %get-tuple-element.17), channel_id=1, source_target_pairs={{0,128},{1,129},{2,130},{3,131},{4,132},{5,133},{6,134},{7,135},{8... | collective-permute-start | bytes 1572872 | tf_op jit(solution)/shard_map/ppermute | solution.py:308
  17.2 15.3 %collective-permute-start.3 = (f32[4,2,2,64,128]{4,3,2,1,0:T(8,128)S(1)}, f32[4,2,2,64,128]{4,3,2,1,0:T(8,128)S(1)}, u32[]{:S(2)}, u32[]{:S(2)}) collective-permute-start(f32[4,2,2,64,128]{4,3,2,1,0:T(8,128)S(1)} %get-tuple-element.18), channel_id=1, source_target_pairs={{0,1},{1,2},{2,3},{3,4},{4,5},{5,6},{6,7},{7,8},{8,9},{9,10},{10,1... | collective-permute-start | bytes 1572872 | tf_op jit(solution)/shard_map/ppermute | solution.py:308
  20.8 23.5 %collective-permute-start.4 = (f32[4,2,2,64,128]{4,3,2,1,0:T(8,128)S(1)}, f32[4,2,2,64,128]{4,3,2,1,0:T(8,128)S(1)}, u32[]{:S(2)}, u32[]{:S(2)}) collective-permute-start(f32[4,2,2,64,128]{4,3,2,1,0:T(8,128)S(1)} %get-tuple-element.19), channel_id=1, source_target_pairs={{0,129},{1,130},{2,131},{3,132},{4,133},{5,134},{6,135},{7,136},{8... | collective-permute-start | bytes 1572872 | tf_op jit(solution)/shard_map/ppermute | solution.py:308
  24.7 19.5 %collective-permute-start.5 = (f32[4,2,2,64,128]{4,3,2,1,0:T(8,128)S(1)}, f32[4,2,2,64,128]{4,3,2,1,0:T(8,128)S(1)}, u32[]{:S(2)}, u32[]{:S(2)}) collective-permute-start(f32[4,2,2,64,128]{4,3,2,1,0:T(8,128)S(1)} %get-tuple-element.20), channel_id=1, source_target_pairs={{1,0},{2,1},{3,2},{4,3},{5,4},{6,5},{7,6},{8,7},{9,8},{10,9},{11,1... | collective-permute-start | bytes 1572872 | tf_op jit(solution)/shard_map/ppermute | solution.py:308
  28.3 27.3 %collective-permute-start.6 = (f32[4,2,2,64,128]{4,3,2,1,0:T(8,128)S(1)}, f32[4,2,2,64,128]{4,3,2,1,0:T(8,128)S(1)}, u32[]{:S(2)}, u32[]{:S(2)}) collective-permute-start(f32[4,2,2,64,128]{4,3,2,1,0:T(8,128)S(1)} %get-tuple-element.21), channel_id=1, source_target_pairs={{1,128},{2,129},{3,130},{4,131},{5,132},{6,133},{7,134},{8,135},{9... | collective-permute-start | bytes 1572872 | tf_op jit(solution)/shard_map/ppermute | solution.py:308
  55.7 56.9 %copy-start.3 = (s32[8]{0:T(128)S(1)}, s32[8]{0:T(128)}, u32[]{:S(2)}) copy-start(s32[8]{0:T(128)} %own_cols.1) | copy-start | bytes 100
  67.7 1.3 collective-permute-start.12
  69.0 3.6 %collective-permute-start.13 = (f32[2,64,128]{2,1,0:T(8,128)S(1)}, f32[2,64,128]{2,1,0:T(8,128)S(1)}, u32[]{:S(2)}, u32[]{:S(2)}) collective-permute-start(f32[2,64,128]{2,1,0:T(8,128)S(1)} %add.24), channel_id=1, source_target_pairs={{0,1},{1,0},{2,3},{3,2},{4,5},{5,4},{6,7},{7,6},{8,9},{9,8},{10,11... | collective-permute-start | bytes 196616 | tf_op jit(solution)/shard_map/ppermute | solution.py:347
  72.6 4.7 %collective-permute-start.14 = (f32[2,64,128]{2,1,0:T(8,128)S(1)}, f32[2,64,128]{2,1,0:T(8,128)S(1)}, u32[]{:S(2)}, u32[]{:S(2)}) collective-permute-start(f32[2,64,128]{2,1,0:T(8,128)S(1)} %add.25), channel_id=1, source_target_pairs={{0,2},{1,3},{2,0},{3,1},{4,6},{5,7},{6,4},{7,5},{8,10},{9,11},{10,... | collective-permute-start | bytes 196616 | tf_op jit(solution)/shard_map/ppermute | solution.py:347
  77.3 3.2 %collective-permute-start.15 = (f32[2,64,128]{2,1,0:T(8,128)S(1)}, f32[2,64,128]{2,1,0:T(8,128)S(1)}, u32[]{:S(2)}, u32[]{:S(2)}) collective-permute-start(f32[2,64,128]{2,1,0:T(8,128)S(1)} %add.26), channel_id=1, source_target_pairs={{0,4},{1,5},{2,6},{3,7},{4,0},{5,1},{6,2},{7,3},{8,12},{9,13},{10,... | collective-permute-start | bytes 196616 | tf_op jit(solution)/shard_map/ppermute | solution.py:347
  80.5 4.7 %collective-permute-start.16 = (f32[2,64,128]{2,1,0:T(8,128)S(1)}, f32[2,64,128]{2,1,0:T(8,128)S(1)}, u32[]{:S(2)}, u32[]{:S(2)}) collective-permute-start(f32[2,64,128]{2,1,0:T(8,128)S(1)} %add.27), channel_id=1, source_target_pairs={{0,8},{1,9},{2,10},{3,11},{4,12},{5,13},{6,14},{7,15},{8,0},{9,1},... | collective-permute-start | bytes 196616 | tf_op jit(solution)/shard_map/ppermute | solution.py:347
  85.3 3.5 %collective-permute-start.17 = (f32[2,64,128]{2,1,0:T(8,128)S(1)}, f32[2,64,128]{2,1,0:T(8,128)S(1)}, u32[]{:S(2)}, u32[]{:S(2)}) collective-permute-start(f32[2,64,128]{2,1,0:T(8,128)S(1)} %add.28), channel_id=1, source_target_pairs={{0,16},{1,17},{2,18},{3,19},{4,20},{5,21},{6,22},{7,23},{8,24},{9,... | collective-permute-start | bytes 196616 | tf_op jit(solution)/shard_map/ppermute | solution.py:347
  88.8 19.8 %collective-permute-start.18 = (f32[2,64,128]{2,1,0:T(8,128)S(1)}, f32[2,64,128]{2,1,0:T(8,128)S(1)}, u32[]{:S(2)}, u32[]{:S(2)}) collective-permute-start(f32[2,64,128]{2,1,0:T(8,128)S(1)} %add.29), channel_id=1, source_target_pairs={{0,32},{1,33},{2,34},{3,35},{4,36},{5,37},{6,38},{7,39},{8,40},{9,... | collective-permute-start | bytes 196616 | tf_op jit(solution)/shard_map/ppermute | solution.py:347
  95.5 17.1 %collective-permute-start.11 = (f32[4,2,2,64,128]{4,3,2,1,0:T(8,128)S(1)}, f32[4,2,2,64,128]{4,3,2,1,0:T(8,128)S(1)}, u32[]{:S(2)}, u32[]{:S(2)}) collective-permute-start(f32[4,2,2,64,128]{4,3,2,1,0:T(8,128)S(1)} %get-tuple-element.27), channel_id=1, source_target_pairs={{0,128},{1,129},{2,130},{3,131},{4,132},{5,133},{6,134},{7,135},{8... | collective-permute-start | bytes 1572872 | tf_op jit(solution)/shard_map/ppermute | solution.py:308
  101.4 15.4 %collective-permute-start.7 = (f32[4,2,2,64,128]{4,3,2,1,0:T(8,128)S(1)}, f32[4,2,2,64,128]{4,3,2,1,0:T(8,128)S(1)}, u32[]{:S(2)}, u32[]{:S(2)}) collective-permute-start(f32[4,2,2,64,128]{4,3,2,1,0:T(8,128)S(1)} %get-tuple-element.22), channel_id=1, source_target_pairs={{0,1},{1,2},{2,3},{3,4},{4,5},{5,6},{6,7},{7,8},{8,9},{9,10},{10,1... | collective-permute-start | bytes 1572872 | tf_op jit(solution)/shard_map/ppermute | solution.py:308
  103.3 25.1 %collective-permute-start.8 = (f32[4,2,2,64,128]{4,3,2,1,0:T(8,128)S(1)}, f32[4,2,2,64,128]{4,3,2,1,0:T(8,128)S(1)}, u32[]{:S(2)}, u32[]{:S(2)}) collective-permute-start(f32[4,2,2,64,128]{4,3,2,1,0:T(8,128)S(1)} %get-tuple-element.23), channel_id=1, source_target_pairs={{0,129},{1,130},{2,131},{3,132},{4,133},{5,134},{6,135},{7,136},{8... | collective-permute-start | bytes 1572872 | tf_op jit(solution)/shard_map/ppermute | solution.py:308
  105.2 23.2 %collective-permute-start.9 = (f32[4,2,2,64,128]{4,3,2,1,0:T(8,128)S(1)}, f32[4,2,2,64,128]{4,3,2,1,0:T(8,128)S(1)}, u32[]{:S(2)}, u32[]{:S(2)}) collective-permute-start(f32[4,2,2,64,128]{4,3,2,1,0:T(8,128)S(1)} %get-tuple-element.24), channel_id=1, source_target_pairs={{1,0},{2,1},{3,2},{4,3},{5,4},{6,5},{7,6},{8,7},{9,8},{10,9},{11,1... | collective-permute-start | bytes 1572872 | tf_op jit(solution)/shard_map/ppermute | solution.py:308
  108.6 30.4 %collective-permute-start.10 = (f32[4,2,2,64,128]{4,3,2,1,0:T(8,128)S(1)}, f32[4,2,2,64,128]{4,3,2,1,0:T(8,128)S(1)}, u32[]{:S(2)}, u32[]{:S(2)}) collective-permute-start(f32[4,2,2,64,128]{4,3,2,1,0:T(8,128)S(1)} %get-tuple-element.25), channel_id=1, source_target_pairs={{1,128},{2,129},{3,130},{4,131},{5,132},{6,133},{7,134},{8,135},{9... | collective-permute-start | bytes 1572872 | tf_op jit(solution)/shard_map/ppermute | solution.py:308
  112.6 29.3 %collective-permute-start.19 = (f32[2,64,128]{2,1,0:T(8,128)S(1)}, f32[2,64,128]{2,1,0:T(8,128)S(1)}, u32[]{:S(2)}, u32[]{:S(2)}) collective-permute-start(f32[2,64,128]{2,1,0:T(8,128)S(1)} %add.30), channel_id=1, source_target_pairs={{0,64},{1,65},{2,66},{3,67},{4,68},{5,69},{6,70},{7,71},{8,72},{9,... | collective-permute-start | bytes 196616 | tf_op jit(solution)/shard_map/ppermute | solution.py:347
where the time goes:
time: 143 us
  waiting for transfers between devices  71.1 us (50%)
  starting transfers between devices  48.3 us (34%)
  Pallas kernels  19.2 us (13%)
  local copies, waits for them, and re-layouts  2.28 us (2%)
    ppermute x13, waiting for transfers between devices, send(): return lax.ppermute(value, AXES, pairs)  51.9 us
    ppermute x13, starting transfers between devices, send(): return lax.ppermute(value, AXES, pairs)  41 us
    pallas_call x5, Pallas kernels, call(): pl.pallas_call(kernel, out_shape=out_shapes if single else tuple(out_shap...  19.2 us
    ppermute x7, waiting for transfers between devices, work(): total = total + lax.ppermute(total, AXES, pairs)  19.2 us
    ppermute x7, starting transfers between devices, work(): total = total + lax.ppermute(total, AXES, pairs)  7.24 us
  transfers between devices with their start and end apart: 20, of which 12 were waited for; matrix products, arithmetic and copies ran while one was open for 0% of the time, Pallas kernels for 5%

commit v1 on v0

--- a/solution.py
+++ b/solution.py
@@ -14,7 +14,7 @@
 AXES = ("depth", "tile")
 F32 = jnp.float32
 BF16 = jnp.bfloat16
-RANK = {1: 0, 2: 1, 4: 2, 8: 3, 16: 4, 32: 5, 64: 6}
+MASKS = (1, 3, 4, 12, 16, 32, 112)
 VMEM = pl.BlockSpec(memory_space=pltpu.VMEM)
 SMEM = pl.BlockSpec(memory_space=pltpu.SMEM)
 
@@ -39,42 +39,47 @@
     return np.stack([*halves(fwd), *halves(inv)]), kern
 
 
+def masks_of(n_tile):
+    if n_tile == 1 << len(MASKS):
+        return MASKS
+    return tuple(1 << k for k in range(n_tile.bit_length() - 1))
+
+
 def window_of(col, cols, size):
     block = jnp.minimum(col // size, cols // size - 2)
     return pl.multiple_of(block * size, size), col - block * size
 
 
-def cut_piece(trans_ref, out_ref, item, col):
-    parts, group, _, cols = trans_ref.shape
+def cut_piece(strip_ref, out_ref, item, col, first):
+    parts, group, _, cols = strip_ref.shape
     size = out_ref.shape[-1]
     base, shift = window_of(col, cols, size)
     for part in range(parts):
         for s in range(group):
-            wide = trans_ref[part, s, :, pl.ds(base, 2 * size)]
+            wide = strip_ref[part, s, :, pl.ds(base, 2 * size)]
             turned = pltpu.roll(wide, lax.rem(2 * size - shift, 2 * size), 1)
-            out_ref[item, part, s] = turned[:, :size]
-
-
-def cut_own_kernel(cols_ref, trans_ref, same_ref, other_ref):
+            out_ref[item, part, first + s] = turned[:, :size]
+
+
+def cut_halo_kernel(cols_ref, mine_ref, theirs_ref, pass_ref, keep_ref):
     depth = lax.axis_index("depth")
-
-    @pl.loop(0, same_ref.shape[0])
+    group = mine_ref.shape[1]
+
+    @pl.loop(0, keep_ref.shape[0])
     def _(item):
-        cut_piece(trans_ref, same_ref, item, cols_ref[2 * item + depth])
-        cut_piece(trans_ref, other_ref, item, cols_ref[2 * item + 1 - depth])
-
-
-def cut_halo_kernel(up_cols_ref, dn_cols_ref, trans_ref, up_same, up_other, dn_same, dn_other):
+        for out_ref, slot in ((pass_ref, 2 * item + 1 - depth), (keep_ref, 2 * item + depth)):
+            cut_piece(mine_ref, out_ref, item, cols_ref[slot], depth * group)
+            cut_piece(theirs_ref, out_ref, item, cols_ref[slot], (1 - depth) * group)
+
+
+def cut_own_kernel(cols_ref, mine_ref, theirs_ref, own_ref):
     depth = lax.axis_index("depth")
-
-    @pl.loop(0, up_same.shape[0])
+    group = mine_ref.shape[1]
+
+    @pl.loop(0, own_ref.shape[0])
     def _(item):
-        same = 2 * item + depth
-        other = 2 * item + 1 - depth
-        cut_piece(trans_ref, up_same, item, up_cols_ref[same])
-        cut_piece(trans_ref, up_other, item, up_cols_ref[other])
-        cut_piece(trans_ref, dn_same, item, dn_cols_ref[same])
-        cut_piece(trans_ref, dn_other, item, dn_cols_ref[other])
+        cut_piece(mine_ref, own_ref, item, cols_ref[2 * item + depth], depth * group)
+        cut_piece(theirs_ref, own_ref, item, cols_ref[2 * item + depth], (1 - depth) * group)
 
 
 def split3(x):
@@ -105,22 +110,17 @@
 def compute_kernel(
     counts_ref,
     rows_ref,
-    own_same,
-    own_other,
-    up_same,
-    up_other,
-    dn_same,
-    dn_other,
+    own,
+    halo_keep,
+    halo_swap,
     probe_ref,
     diff_ref,
     dft_ref,
     kern_ref,
-    g_own_same,
-    g_own_other,
-    g_up_same,
-    g_up_other,
-    g_dn_same,
-    g_dn_other,
+    g_own,
+    g_pass,
+    g_keep,
+    g_cross,
     p_same,
     p_other,
     stack,
@@ -132,17 +132,15 @@
 ):
     depth, tile = lax.axis_index("depth"), lax.axis_index("tile")
     filled = counts_ref[tile]
-    items, parts, per, strip, size = own_same.shape
+    items, parts, slices, strip, size = own.shape
+    per = slices // 2
     pairs = range(items // 2)
-    slices = 2 * per
     half = size // 2
     mine, theirs = depth * per, (1 - depth) * per
     slots = [2 * item + depth for item in range(items)]
-    outs = (
-        (g_up_same, g_up_other, 0, half),
-        (g_own_same, g_own_other, half, strip),
-        (g_dn_same, g_dn_other, half + strip, half),
-    )
+    far = half + strip
+    from_keep, from_swap = pl.multiple_of(depth * far, half), pl.multiple_of((1 - depth) * far, half)
+    to_send, to_cross = from_swap, from_keep
     live = [(slot < filled).astype(F32) for slot in slots]
     kc = jnp.concatenate([kern_ref[0], kern_ref[0]], axis=0)
     ks = jnp.concatenate([kern_ref[1], kern_ref[1]], axis=0)
@@ -151,14 +149,10 @@
         offset = rows_ref[slots[item]] - (tile * strip - half)
         p, q = item // 2, item % 2
         for part in range(parts):
-            for s in range(per):
-                for base, same, other, at, length in (
-                    (0, up_same, up_other, strip - half, half),
-                    (half, own_same, own_other, 0, strip),
-                    (half + strip, dn_same, dn_other, 0, half),
-                ):
-                    stack[mine + s, pl.ds(base, length), :] = same[item, part, s, at : at + length]
-                    stack[theirs + s, pl.ds(base, length), :] = other[item, part, s, at : at + length]
+            for s in range(slices):
+                stack[s, pl.ds(from_keep, half), :] = halo_keep[item, part, s]
+                stack[s, half : half + strip, :] = own[item, part, s]
+                stack[s, pl.ds(from_swap, half), :] = halo_swap[item, part, s]
             for s in range(slices):
                 trans[p, s, part * size : (part + 1) * size, q * size : (q + 1) * size] = stack[
                     s, pl.ds(offset, size), :
@@ -231,9 +225,12 @@
                     p, s, part * size : (part + 1) * size, q * size : (q + 1) * size
                 ]
             for s in range(per):
-                for same, other, base, length in outs:
-                    same[item, part, s] = grads[mine + s, base : base + length]
-                    other[item, part, s] = grads[theirs + s, base : base + length]
+                g_own[item, part, s] = grads[mine + s, half : half + strip]
+                g_pass[0, item, part, s] = grads[theirs + s, pl.ds(to_send, half), :]
+                g_keep[0, item, part, s] = grads[mine + s, pl.ds(to_send, half), :]
+                g_cross[0, item, part, s] = grads[theirs + s, half : half + strip]
+                g_cross[1, item, part, s] = grads[mine + s, pl.ds(to_cross, half), :]
+                g_cross[2, item, part, s] = grads[theirs + s, pl.ds(to_cross, half), :]
 
 
 def add_blocks(out_ref, cols_ref, filled, block_ref, parity):
@@ -254,25 +251,26 @@
                     out_ref[part, s, :, pl.ds(base, 2 * size)] += pltpu.roll(wide, shift, 1)
 
 
-def place_own_kernel(counts_ref, own_cols, own_same, own_other, out_ref):
+def place_own_kernel(counts_ref, own_cols, own_same, crossed, out_ref):
     depth, tile = lax.axis_index("depth"), lax.axis_index("tile")
     out_ref[...] = jnp.zeros_like(out_ref)
     add_blocks(out_ref, own_cols, counts_ref[tile], own_same, depth)
-    add_blocks(out_ref, own_cols, counts_ref[tile], own_other, 1 - depth)
-
-
-def place_halo_kernel(
-    counts_ref, up_cols, dn_cols, up_same, up_other, dn_same, dn_other, so_far, out_ref
-):
+    add_blocks(out_ref, own_cols, counts_ref[tile], crossed.at[0], 1 - depth)
+
+
+def place_halo_kernel(counts_ref, keep_cols, swap_cols, keep, swap_in, so_far, out_ref):
     depth, tile = lax.axis_index("depth"), lax.axis_index("tile")
     last = counts_ref.shape[0] - 1
-    above = jnp.where(tile > 0, counts_ref[jnp.maximum(tile - 1, 0)], 0)
-    below = jnp.where(tile < last, counts_ref[jnp.minimum(tile + 1, last)], 0)
+
+    def filled(at):
+        return jnp.where((at >= 0) & (at <= last), counts_ref[jnp.clip(at, 0, last)], 0)
+
+    by = 1 - 2 * depth
     out_ref[...] = so_far[...]
-    add_blocks(out_ref, up_cols, above, up_same, depth)
-    add_blocks(out_ref, up_cols, above, up_other, 1 - depth)
-    add_blocks(out_ref, dn_cols, below, dn_same, depth)
-    add_blocks(out_ref, dn_cols, below, dn_other, 1 - depth)
+    add_blocks(out_ref, keep_cols, filled(tile - by), keep.at[0], depth)
+    add_blocks(out_ref, keep_cols, filled(tile - by), keep.at[1], 1 - depth)
+    add_blocks(out_ref, swap_cols, filled(tile + by), swap_in.at[0], 1 - depth)
+    add_blocks(out_ref, swap_cols, filled(tile + by), swap_in.at[1], depth)
 
 
 def call(kernel, in_specs, out_shapes, args, scratch=(), cost=(1 << 20, 1 << 20), aliases=None, limit=16):
@@ -298,32 +296,33 @@
     slices = n_depth * per
     items = slots // n_depth
 
-    def send(value, cross, by):
-        pairs = [
-            (d * n_tile + t, (d + cross) % n_depth * n_tile + t + by)
-            for d in range(n_depth)
-            for t in range(n_tile)
-            if 0 <= t + by < n_tile
-        ]
+    swaps = [(d * n_tile + t, (1 - d) * n_tile + t) for d in range(n_depth) for t in range(n_tile)]
+    moves = [(t, t + 1) for t in range(n_tile - 1)] + [(n_tile + t + 1, n_tile + t) for t in range(n_tile - 1)]
+    asks = [(b, a) for a, b in moves]
+
+    def send(value, pairs):
         return lax.ppermute(value, AXES, pairs)
 
-    up_cols = send(scan_cols, 0, 1)
-    dn_cols = send(scan_cols, 0, -1)
-    bank = jax.ShapeDtypeStruct((items, parts, per, strip, size), F32)
-    own_same, own_cross = call(
-        cut_own_kernel, [SMEM, VMEM], [bank, bank], (scan_cols, transmission)
-    )
-    own_other = send(own_cross, 1, 0)
-    up_s, up_x, dn_s, dn_x = call(
-        cut_halo_kernel, [SMEM, SMEM, VMEM], [bank] * 4, (up_cols, dn_cols, transmission)
-    )
-    halos = (send(dn_s, 0, 1), send(dn_x, 1, 1), send(up_s, 0, -1), send(up_x, 1, -1))
-
+    swap_cols = send(scan_cols, asks)
+    theirs = send(transmission, swaps)
+    bank = jax.ShapeDtypeStruct((items, parts, slices, strip, size), F32)
+    cut_pass, cut_keep = call(
+        cut_halo_kernel, [SMEM, VMEM, VMEM], [bank] * 2, (swap_cols, transmission, theirs)
+    )
+    passed = send(cut_pass, moves)
+    halo_keep = send(cut_keep, moves)
+    halo_swap = send(passed, swaps)
+    keep_cols = send(swap_cols, swaps)
+    own = call(cut_own_kernel, [SMEM, VMEM, VMEM], bank, (scan_cols, transmission, theirs))
+
+    piece = jax.ShapeDtypeStruct((items, parts, per, strip, size), F32)
+    both = jax.ShapeDtypeStruct((n_depth, items, parts, per, half, size), F32)
+    crossing = jax.ShapeDtypeStruct((3, items, parts, per, half, size), F32)
     results = call(
         compute_kernel,
-        [SMEM, SMEM] + [VMEM] * 10,
-        [bank] * 6 + [jax.ShapeDtypeStruct((parts, half, size), F32)] * 2,
-        (tile_counts, scan_rows, own_same, own_other, *halos, probe, diffraction)
+        [SMEM, SMEM] + [VMEM] * 7,
+        [piece, both, both, crossing] + [jax.ShapeDtypeStruct((parts, half, size), F32)] * 2,
+        (tile_counts, scan_rows, own, halo_keep, halo_swap, probe, diffraction)
         + tuple(jnp.asarray(v) for v in tables(size)),
         scratch=[
             pltpu.VMEM((slices, 2 * half + strip, size), F32),
@@ -336,32 +335,31 @@
         cost=(6 << 30, 8 << 20),
         limit=24,
     )
-    g_own_s, g_own_x, g_up_s, g_up_x, g_dn_s, g_dn_x, p_same, p_other = results
-
-    total = p_same + send(p_other, 1, 0)
-    own_back = send(g_own_x, 1, 0)
-    steps = [1 << k for k in range(n_tile.bit_length() - 1)]
-    order = sorted(steps, key=lambda step: RANK.get(step, 0))
-    for step in order:
-        pairs = [(d * n_tile + t, d * n_tile + (t ^ step)) for d in range(n_depth) for t in range(n_tile)]
+    g_own, g_pass, g_keep, g_cross, p_same, p_other = results
+
+    total = p_same + send(p_other, swaps)
+    crossed = send(g_cross, swaps)
+    for mask in masks_of(n_tile):
+        pairs = [(d * n_tile + t, d * n_tile + (t ^ mask)) for d in range(n_depth) for t in range(n_tile)]
         total = total + lax.ppermute(total, AXES, pairs)
-    up_same = send(g_dn_s, 0, 1)
-    up_other = send(g_dn_x, 1, 1)
-    dn_same = send(g_up_s, 0, -1)
-    dn_other = send(g_up_x, 1, -1)
+    g_pass = lax.dynamic_update_slice(g_pass, crossed[1:2], (1, 0, 0, 0, 0, 0))
+    g_keep = lax.dynamic_update_slice(g_keep, crossed[2:3], (1, 0, 0, 0, 0, 0))
+    arrived = send(g_pass, moves)
+    keep = send(g_keep, moves)
+    swap_in = send(arrived, swaps)
 
     grad_shape = jax.ShapeDtypeStruct(transmission.shape, F32)
     grad = call(
         place_own_kernel,
         [SMEM] * 2 + [VMEM] * 2,
         grad_shape,
-        (tile_counts, scan_cols, g_own_s, own_back),
+        (tile_counts, scan_cols, g_own, crossed),
     )
     grad = call(
         place_halo_kernel,
-        [SMEM] * 3 + [VMEM] * 5,
+        [SMEM] * 3 + [VMEM] * 3,
         grad_shape,
-        (tile_counts, up_cols, dn_cols, up_same, up_other, dn_same, dn_other, grad),
+        (tile_counts, keep_cols, swap_cols, keep, swap_in, grad),
     )
     return (grad, total)
 

time: 143 us -> 128 us (0.90)
  the two profiles are of different devices: /device:TPU:63 before, /device:TPU:2 now
where the time goes in v1:
time: 128 us; the launch traced here: 127 us
  waiting for transfers between devices  57 us (45%)
  starting transfers between devices  47.6 us (37%)
  Pallas kernels  18.9 us (15%)
  local copies, waits for them, and re-layouts  1.71 us (1%)
    ppermute x11, waiting for transfers between devices, send(): return lax.ppermute(value, AXES, pairs)  32.8 us
    ppermute x7, starting transfers between devices, work(): total = total + lax.ppermute(total, AXES, pairs)  25.4 us
    ppermute x7, waiting for transfers between devices, work(): total = total + lax.ppermute(total, AXES, pairs)  24.2 us
    ppermute x11, starting transfers between devices, send(): return lax.ppermute(value, AXES, pairs)  22.2 us
    pallas_call x5, Pallas kernels, call(): pl.pallas_call(kernel, out_shape=out_shapes if single else tuple(out_shap...  18.9 us
  transfers between devices with their start and end apart: 18, of which 13 were waited for; matrix products, arithmetic and copies ran while one was open for 1% of the time, Pallas kernels for 2%

profile of v1, /device:TPU:2, one launch (start us, length us, event | category | flops | bytes accessed | tf_op | source)
XLA Modules:
  0.0 126.9 jit_solution(6092379422280146259)
XLA Ops:
  0.6 0.1 collective-permute-start.2
  0.7 4.2 %collective-permute-start = (s32[8]{0:T(128)}, s32[8]{0:T(128)S(1)}, u32[]{:S(2)}, u32[]{:S(2)}) collective-permute-start(s32[8]{0:T(128)} %own_cols.1), channel_id=1, source_target_pairs={{1,0},{2,1},{3,2},{4,3},{5,4},{6,5},{7,6},{8,7},{9,8},{10,9},{11,1... | collective-permute-start | bytes 104 | tf_op jit(solution)/shard_map/ppermute | solution.py:304
  4.9 1.4 %collective-permute-done.cols_ref.swap_cols = s32[8]{0:T(128)S(1)} collective-permute-done((s32[8]{0:T(128)}, s32[8]{0:T(128)S(1)}, u32[]{:S(2)}, u32[]{:S(2)}) %collective-permute-start) | collective-permute-done | bytes 64 | tf_op jit(solution)/shard_map/ppermute | solution.py:304
  6.3 0.0 collective-permute-done.2.theirs_ref
  6.3 1.6 %copy-done = f32[2,2,64,2048]{3,2,1,0:T(8,128)S(1)} copy-done((f32[2,2,64,2048]{3,2,1,0:T(8,128)S(1)}, f32[2,2,64,2048]{3,2,1,0:T(8,128)}, u32[]{:S(2)}) %copy-start) | copy-done | bytes 2097176
  7.9 1.9 %shard_map.96 = (f32[4,2,4,64,128]{4,3,2,1,0:T(8,128)S(1)}, f32[4,2,4,64,128]{4,3,2,1,0:T(8,128)S(1)}) custom-call(s32[8]{0:T(128)S(1)} %collective-permute-done.cols_ref.swap_cols, f32[2,2,64,2048]{3,2,1,0:T(8,128)S(1)} %copy-done, f32[2,2,64,2048]{3,2,1,0:T(8,128)S(1)} %collective-permute-done.2.theirs_ref), custom_call_target="tpu_custom_call" | custom-call | flops 1048576 | bytes 1048576 | tf_op jit(solution)/shard_map/pallas_call | solution.py:278
  9.9 3.4 %collective-permute-start.4 = (f32[4,2,4,64,128]{4,3,2,1,0:T(8,128)S(1)}, f32[4,2,4,64,128]{4,3,2,1,0:T(8,128)S(1)}, u32[]{:S(2)}, u32[]{:S(2)}) collective-permute-start(f32[4,2,4,64,128]{4,3,2,1,0:T(8,128)S(1)} %get-tuple-element.11), channel_id=1, source_target_pairs={{0,1},{1,2},{2,3},{3,4},{4,5},{5,6},{6,7},{7,8},{8,9},{9,10},{10,1... | collective-permute-start | bytes 3145736 | tf_op jit(solution)/shard_map/ppermute | solution.py:304
  13.3 0.0 copy-start.2
  13.3 0.0 copy-start.4
  13.3 0.0 copy-start.5
  13.3 0.0 copy-start.6
  13.3 0.0 copy-start.7
  13.3 0.0 copy-start.8
  13.4 5.3 %collective-permute-start.3 = (f32[4,2,4,64,128]{4,3,2,1,0:T(8,128)S(1)}, f32[4,2,4,64,128]{4,3,2,1,0:T(8,128)S(1)}, u32[]{:S(2)}, u32[]{:S(2)}) collective-permute-start(f32[4,2,4,64,128]{4,3,2,1,0:T(8,128)S(1)} %get-tuple-element.10), channel_id=1, source_target_pairs={{0,1},{1,2},{2,3},{3,4},{4,5},{5,6},{6,7},{7,8},{8,9},{9,10},{10,1... | collective-permute-start | bytes 3145736 | tf_op jit(solution)/shard_map/ppermute | solution.py:304
  18.7 7.9 %collective-permute-done.4 = f32[4,2,4,64,128]{4,3,2,1,0:T(8,128)S(1)} collective-permute-done((f32[4,2,4,64,128]{4,3,2,1,0:T(8,128)S(1)}, f32[4,2,4,64,128]{4,3,2,1,0:T(8,128)S(1)}, u32[]{:S(2)}, u32[]{:S(2)}) %collective-permute-start.4) | collective-permute-done | bytes 1048608 | tf_op jit(solution)/shard_map/ppermute | solution.py:304
  26.6 0.0 collective-permute-start.5
  26.6 1.4 %shard_map.95.own = f32[4,2,4,64,128]{4,3,2,1,0:T(8,128)S(1)} custom-call(s32[8]{0:T(128)S(1)} %copy-done.3, f32[2,2,64,2048]{3,2,1,0:T(8,128)S(1)} %copy-done.1, f32[2,2,64,2048]{3,2,1,0:T(8,128)S(1)} %collective-permute-done.2.theirs_ref), custom_call_target="tpu_custom_call" | custom-call | flops 1048576 | bytes 1048576 | tf_op jit(solution)/shard_map/pallas_call | solution.py:278
  28.0 9.8 %collective-permute-done.3.halo_keep = f32[4,2,4,64,128]{4,3,2,1,0:T(8,128)S(1)} collective-permute-done((f32[4,2,4,64,128]{4,3,2,1,0:T(8,128)S(1)}, f32[4,2,4,64,128]{4,3,2,1,0:T(8,128)S(1)}, u32[]{:S(2)}, u32[]{:S(2)}) %collective-permute-start.3) | collective-permute-done | bytes 1048608 | tf_op jit(solution)/shard_map/ppermute | solution.py:304
  37.8 0.0 collective-permute-done.5.halo_swap
  37.9 11.8 %shard_map.97 = (f32[4,2,2,64,128]{4,3,2,1,0:T(8,128)S(1)}, f32[2,4,2,2,64,128]{5,4,3,2,1,0:T(8,128)S(1)}, f32[2,4,2,2,64,128]{5,4,3,2,1,0:T(8,128)S(1)}, f32[3,...) custom-call(s32[128]{0:T(128)S(1)} %copy-done.2, s32[8]{0:T(128)S(1)} %copy-done.6, ...), custom_call_target="tpu_custom_call" | custom-call | flops 6442450944 | bytes 8388608 | tf_op jit(solution)/shard_map/pallas_call | solution.py:278
  49.7 0.1 collective-permute-start.6
  49.8 3.4 %collective-permute-done.6.crossed = f32[3,4,2,2,64,128]{5,4,3,2,1,0:T(8,128)S(1)} collective-permute-done((f32[3,4,2,2,64,128]{5,4,3,2,1,0:T(8,128)S(1)}, f32[3,4,2,2,64,128]{5,4,3,2,1,0:T(8,128)S(1)}, u32[]{:S(2)}, u32[]{:S(2)}) %collective-permute-start.6) | collective-permute-done | bytes 1572896 | tf_op jit(solution)/shard_map/ppermute | solution.py:304
  53.2 0.1 slice_dynamic-update-slice_fusion
  53.3 4.2 %collective-permute-start.8 = (f32[2,4,2,2,64,128]{5,4,3,2,1,0:T(8,128)S(1)}, f32[2,4,2,2,64,128]{5,4,3,2,1,0:T(8,128)S(1)}, u32[]{:S(2)}, u32[]{:S(2)}) collective-permute-start(f32[2,4,2,2,64,128]{5,4,3,2,1,0:T(8,128)S(1)} %get-tuple-element.18), channel_id=1, source_target_pairs={{0,1},{1,2},{2,3},{3,4},{4,5},{5,6},{6,7},{7,8},{8,9},{9,10},{10,1... | collective-permute-start | bytes 3145736 | tf_op jit(solution)/shard_map/ppermute | solution.py:304
  57.5 4.4 %collective-permute-start.7 = (f32[2,4,2,2,64,128]{5,4,3,2,1,0:T(8,128)S(1)}, f32[2,4,2,2,64,128]{5,4,3,2,1,0:T(8,128)S(1)}, u32[]{:S(2)}, u32[]{:S(2)}) collective-permute-start(f32[2,4,2,2,64,128]{5,4,3,2,1,0:T(8,128)S(1)} %get-tuple-element.19), channel_id=1, source_target_pairs={{0,1},{1,2},{2,3},{3,4},{4,5},{5,6},{6,7},{7,8},{8,9},{9,10},{10,1... | collective-permute-start | bytes 3145736 | tf_op jit(solution)/shard_map/ppermute | solution.py:304
  61.9 8.1 %collective-permute-done.8 = f32[2,4,2,2,64,128]{5,4,3,2,1,0:T(8,128)S(1)} collective-permute-done((f32[2,4,2,2,64,128]{5,4,3,2,1,0:T(8,128)S(1)}, f32[2,4,2,2,64,128]{5,4,3,2,1,0:T(8,128)S(1)}, u32[]{:S(2)}, u32[]{:S(2)}) %collective-permute-start.8) | collective-permute-done | bytes 1048608 | tf_op jit(solution)/shard_map/ppermute | solution.py:304
  70.0 0.0 collective-permute-start.9
  70.0 0.5 collective-permute-start.10
  70.5 2.2 %collective-permute-done.10 = f32[2,64,128]{2,1,0:T(8,128)S(1)} collective-permute-done((f32[2,64,128]{2,1,0:T(8,128)S(1)}, f32[2,64,128]{2,1,0:T(8,128)S(1)}, u32[]{:S(2)}, u32[]{:S(2)}) %collective-permute-start.10) | collective-permute-done | bytes 65568 | tf_op jit(solution)/shard_map/ppermute | solution.py:304
  72.7 0.1 collective-permute-start.11
  72.8 9.8 %collective-permute-done.11 = f32[2,64,128]{2,1,0:T(8,128)S(1)} collective-permute-done((f32[2,64,128]{2,1,0:T(8,128)S(1)}, f32[2,64,128]{2,1,0:T(8,128)S(1)}, u32[]{:S(2)}, u32[]{:S(2)}) %collective-permute-start.11) | collective-permute-done | bytes 65568 | tf_op jit(solution)/shard_map/ppermute | solution.py:344
  82.6 2.4 %collective-permute-start.12 = (f32[2,64,128]{2,1,0:T(8,128)S(1)}, f32[2,64,128]{2,1,0:T(8,128)S(1)}, u32[]{:S(2)}, u32[]{:S(2)}) collective-permute-start(f32[2,64,128]{2,1,0:T(8,128)S(1)} %add.25), channel_id=1, source_target_pairs={{0,3},{1,2},{2,1},{3,0},{4,7},{5,6},{6,5},{7,4},{8,11},{9,10},{10,... | collective-permute-start | bytes 196616 | tf_op jit(solution)/shard_map/ppermute | solution.py:344
  85.0 2.2 %collective-permute-done.12 = f32[2,64,128]{2,1,0:T(8,128)S(1)} collective-permute-done((f32[2,64,128]{2,1,0:T(8,128)S(1)}, f32[2,64,128]{2,1,0:T(8,128)S(1)}, u32[]{:S(2)}, u32[]{:S(2)}) %collective-permute-start.12) | collective-permute-done | bytes 65568 | tf_op jit(solution)/shard_map/ppermute | solution.py:344
  87.3 2.6 %collective-permute-start.13 = (f32[2,64,128]{2,1,0:T(8,128)S(1)}, f32[2,64,128]{2,1,0:T(8,128)S(1)}, u32[]{:S(2)}, u32[]{:S(2)}) collective-permute-start(f32[2,64,128]{2,1,0:T(8,128)S(1)} %add.26), channel_id=1, source_target_pairs={{0,4},{1,5},{2,6},{3,7},{4,0},{5,1},{6,2},{7,3},{8,12},{9,13},{10,... | collective-permute-start | bytes 196616 | tf_op jit(solution)/shard_map/ppermute | solution.py:344
  89.9 2.2 %collective-permute-done.13 = f32[2,64,128]{2,1,0:T(8,128)S(1)} collective-permute-done((f32[2,64,128]{2,1,0:T(8,128)S(1)}, f32[2,64,128]{2,1,0:T(8,128)S(1)}, u32[]{:S(2)}, u32[]{:S(2)}) %collective-permute-start.13) | collective-permute-done | bytes 65568 | tf_op jit(solution)/shard_map/ppermute | solution.py:344
  92.2 4.7 %collective-permute-start.14 = (f32[2,64,128]{2,1,0:T(8,128)S(1)}, f32[2,64,128]{2,1,0:T(8,128)S(1)}, u32[]{:S(2)}, u32[]{:S(2)}) collective-permute-start(f32[2,64,128]{2,1,0:T(8,128)S(1)} %add.27), channel_id=1, source_target_pairs={{0,12},{1,13},{2,14},{3,15},{4,8},{5,9},{6,10},{7,11},{8,4},{9,5},... | collective-permute-start | bytes 196616 | tf_op jit(solution)/shard_map/ppermute | solution.py:344
  96.8 2.2 %collective-permute-done.14 = f32[2,64,128]{2,1,0:T(8,128)S(1)} collective-permute-done((f32[2,64,128]{2,1,0:T(8,128)S(1)}, f32[2,64,128]{2,1,0:T(8,128)S(1)}, u32[]{:S(2)}, u32[]{:S(2)}) %collective-permute-start.14) | collective-permute-done | bytes 65568 | tf_op jit(solution)/shard_map/ppermute | solution.py:344
  99.1 5.3 %collective-permute-start.15 = (f32[2,64,128]{2,1,0:T(8,128)S(1)}, f32[2,64,128]{2,1,0:T(8,128)S(1)}, u32[]{:S(2)}, u32[]{:S(2)}) collective-permute-start(f32[2,64,128]{2,1,0:T(8,128)S(1)} %add.28), channel_id=1, source_target_pairs={{0,16},{1,17},{2,18},{3,19},{4,20},{5,21},{6,22},{7,23},{8,24},{9,... | collective-permute-start | bytes 196616 | tf_op jit(solution)/shard_map/ppermute | solution.py:344
  104.4 2.5 %collective-permute-done.15 = f32[2,64,128]{2,1,0:T(8,128)S(1)} collective-permute-done((f32[2,64,128]{2,1,0:T(8,128)S(1)}, f32[2,64,128]{2,1,0:T(8,128)S(1)}, u32[]{:S(2)}, u32[]{:S(2)}) %collective-permute-start.15) | collective-permute-done | bytes 65568 | tf_op jit(solution)/shard_map/ppermute | solution.py:344
  106.9 3.2 %collective-permute-start.16 = (f32[2,64,128]{2,1,0:T(8,128)S(1)}, f32[2,64,128]{2,1,0:T(8,128)S(1)}, u32[]{:S(2)}, u32[]{:S(2)}) collective-permute-start(f32[2,64,128]{2,1,0:T(8,128)S(1)} %add.29), channel_id=1, source_target_pairs={{0,32},{1,33},{2,34},{3,35},{4,36},{5,37},{6,38},{7,39},{8,40},{9,... | collective-permute-start | bytes 196616 | tf_op jit(solution)/shard_map/ppermute | solution.py:344
  110.1 2.2 %collective-permute-done.16 = f32[2,64,128]{2,1,0:T(8,128)S(1)} collective-permute-done((f32[2,64,128]{2,1,0:T(8,128)S(1)}, f32[2,64,128]{2,1,0:T(8,128)S(1)}, u32[]{:S(2)}, u32[]{:S(2)}) %collective-permute-start.16) | collective-permute-done | bytes 65568 | tf_op jit(solution)/shard_map/ppermute | solution.py:344
  112.4 7.1 %collective-permute-start.17 = (f32[2,64,128]{2,1,0:T(8,128)S(1)}, f32[2,64,128]{2,1,0:T(8,128)S(1)}, u32[]{:S(2)}, u32[]{:S(2)}) collective-permute-start(f32[2,64,128]{2,1,0:T(8,128)S(1)} %add.30), channel_id=1, source_target_pairs={{0,112},{1,113},{2,114},{3,115},{4,116},{5,117},{6,118},{7,119},{8... | collective-permute-start | bytes 196616 | tf_op jit(solution)/shard_map/ppermute | solution.py:344
  119.5 0.0 collective-permute-start.1
  119.5 2.9 %collective-permute-done.17 = f32[2,64,128]{2,1,0:T(8,128)S(1)} collective-permute-done((f32[2,64,128]{2,1,0:T(8,128)S(1)}, f32[2,64,128]{2,1,0:T(8,128)S(1)}, u32[]{:S(2)}, u32[]{:S(2)}) %collective-permute-start.17) | collective-permute-done | bytes 65568 | tf_op jit(solution)/shard_map/ppermute | solution.py:344
  122.5 0.6 add.31
  123.1 1.0 shard_map.98.so_far
  124.1 0.0 collective-permute-done.7.keep
  124.1 2.8 %shard_map.99 = f32[2,2,64,2048]{3,2,1,0:T(8,128)} custom-call(s32[128]{0:T(128)S(1)} %copy-done.2, s32[8]{0:T(128)S(1)} %collective-permute-done.1.keep_cols, s32[8]{0:T(128)S(1)} %collective-permute-done.cols_ref.swap_cols, f32[2,4,2,2,64,128]{5,4,3,2,1,0:T(8,128)S(1)} %collective-permute-done.7.keep, ...), custom_call_target="tpu_custom_call" | custom-call | flops 1048576 | bytes 1048576 | tf_op jit(solution)/shard_map/pallas_call | solution.py:278
  (20 shorter events, 0.1 us)
Async XLA Ops:
  0.6 5.7 %collective-permute-start.2 = (f32[2,2,64,2048]{3,2,1,0:T(8,128)}, f32[2,2,64,2048]{3,2,1,0:T(8,128)S(1)}, u32[]{:S(2)}, u32[]{:S(2)}) collective-permute-start(f32[2,2,64,2048]{3,2,1,0:T(8,128)} %mine_ref.3), channel_id=1, source_target_pairs={{0,128},{1,129},{2,130},{3,131},{4,132},{5,133},{6,134},{7,135},{8... | collective-permute-start | bytes 6291464 | tf_op jit(solution)/shard_map/ppermute | solution.py:304
  0.7 5.6 %collective-permute-start = (s32[8]{0:T(128)}, s32[8]{0:T(128)S(1)}, u32[]{:S(2)}, u32[]{:S(2)}) collective-permute-start(s32[8]{0:T(128)} %own_cols.1), channel_id=1, source_target_pairs={{1,0},{2,1},{3,2},{4,3},{5,4},{6,5},{7,6},{8,7},{9,8},{10,9},{11,1... | collective-permute-start | bytes 104 | tf_op jit(solution)/shard_map/ppermute | solution.py:304
  6.3 1.6 %copy-start = (f32[2,2,64,2048]{3,2,1,0:T(8,128)S(1)}, f32[2,2,64,2048]{3,2,1,0:T(8,128)}, u32[]{:S(2)}) copy-start(f32[2,2,64,2048]{3,2,1,0:T(8,128)} %mine_ref.3) | copy-start | bytes 6291460
  7.9 18.7 %copy-start.1 = (f32[2,2,64,2048]{3,2,1,0:T(8,128)S(1)}, f32[2,2,64,2048]{3,2,1,0:T(8,128)}, u32[]{:S(2)}) copy-start(f32[2,2,64,2048]{3,2,1,0:T(8,128)} %mine_ref.3) | copy-start | bytes 6291460
  7.9 18.7 %copy-start.3 = (s32[8]{0:T(128)S(1)}, s32[8]{0:T(128)}, u32[]{:S(2)}) copy-start(s32[8]{0:T(128)} %own_cols.1) | copy-start | bytes 100
  9.9 16.7 %collective-permute-start.4 = (f32[4,2,4,64,128]{4,3,2,1,0:T(8,128)S(1)}, f32[4,2,4,64,128]{4,3,2,1,0:T(8,128)S(1)}, u32[]{:S(2)}, u32[]{:S(2)}) collective-permute-start(f32[4,2,4,64,128]{4,3,2,1,0:T(8,128)S(1)} %get-tuple-element.11), channel_id=1, source_target_pairs={{0,1},{1,2},{2,3},{3,4},{4,5},{5,6},{6,7},{7,8},{8,9},{9,10},{10,1... | collective-permute-start | bytes 3145736 | tf_op jit(solution)/shard_map/ppermute | solution.py:304
  13.3 24.5 %copy-start.2 = (s32[128]{0:T(128)S(1)}, s32[128]{0:T(128)}, u32[]{:S(2)}) copy-start(s32[128]{0:T(128)} %counts_ref.5) | copy-start | bytes 1540
  13.3 24.5 %copy-start.4 = (f32[8,128,128]{2,1,0:T(8,128)S(1)}, f32[8,128,128]{2,1,0:T(8,128)}, u32[]{:S(2)}) copy-start(f32[8,128,128]{2,1,0:T(8,128)} %diff_ref.1) | copy-start | bytes 1572868
  13.3 24.5 %copy-start.5 = (f32[2,128,128]{2,1,0:T(8,128)S(1)}, f32[2,128,128]{2,1,0:T(8,128)}, u32[]{:S(2)}) copy-start(f32[2,128,128]{2,1,0:T(8,128)} %probe_ref.1) | copy-start | bytes 393220
  13.3 24.5 %copy-start.6 = (s32[8]{0:T(128)S(1)}, s32[8]{0:T(128)}, u32[]{:S(2)}) copy-start(s32[8]{0:T(128)} %rows_ref.1) | copy-start | bytes 100
  13.3 24.5 %copy-start.7 = (bf16[4,256,256]{2,1,0:T(8,128)(2,1)S(1)}, bf16[4,256,256]{2,1,0:T(8,128)(2,1)}, u32[]{:S(2)}) copy-start(bf16[4,256,256]{2,1,0:T(8,128)(2,1)} %constant.8.clone.dft_ref) | copy-start | bytes 1572868
  13.3 24.5 %copy-start.8 = (f32[2,128,128]{2,1,0:T(8,128)S(1)}, f32[2,128,128]{2,1,0:T(8,128)}, u32[]{:S(2)}) copy-start(f32[2,128,128]{2,1,0:T(8,128)} %constant.9.clone.kern_ref) | copy-start | bytes 393220
  13.4 24.4 %collective-permute-start.3 = (f32[4,2,4,64,128]{4,3,2,1,0:T(8,128)S(1)}, f32[4,2,4,64,128]{4,3,2,1,0:T(8,128)S(1)}, u32[]{:S(2)}, u32[]{:S(2)}) collective-permute-start(f32[4,2,4,64,128]{4,3,2,1,0:T(8,128)S(1)} %get-tuple-element.10), channel_id=1, source_target_pairs={{0,1},{1,2},{2,3},{3,4},{4,5},{5,6},{6,7},{7,8},{8,9},{9,10},{10,1... | collective-permute-start | bytes 3145736 | tf_op jit(solution)/shard_map/ppermute | solution.py:304
  26.6 11.2 %collective-permute-start.5 = (f32[4,2,4,64,128]{4,3,2,1,0:T(8,128)S(1)}, f32[4,2,4,64,128]{4,3,2,1,0:T(8,128)S(1)}, u32[]{:S(2)}, u32[]{:S(2)}) collective-permute-start(f32[4,2,4,64,128]{4,3,2,1,0:T(8,128)S(1)} %collective-permute-done.4), channel_id=1, source_target_pairs={{0,128},{1,129},{2,130},{3,131},{4,132},{5,133},{6,134},{7,135},{8... | collective-permute-start | bytes 3145736 | tf_op jit(solution)/shard_map/ppermute | solution.py:304
  49.7 3.5 %collective-permute-start.6 = (f32[3,4,2,2,64,128]{5,4,3,2,1,0:T(8,128)S(1)}, f32[3,4,2,2,64,128]{5,4,3,2,1,0:T(8,128)S(1)}, u32[]{:S(2)}, u32[]{:S(2)}) collective-permute-start(f32[3,4,2,2,64,128]{5,4,3,2,1,0:T(8,128)S(1)} %get-tuple-element.13), channel_id=1, source_target_pairs={{0,128},{1,129},{2,130},{3,131},{4,132},{5,133},{6,134},{7,135},{8... | collective-permute-start | bytes 4718600 | tf_op jit(solution)/shard_map/ppermute | solution.py:304
  53.3 16.7 %collective-permute-start.8 = (f32[2,4,2,2,64,128]{5,4,3,2,1,0:T(8,128)S(1)}, f32[2,4,2,2,64,128]{5,4,3,2,1,0:T(8,128)S(1)}, u32[]{:S(2)}, u32[]{:S(2)}) collective-permute-start(f32[2,4,2,2,64,128]{5,4,3,2,1,0:T(8,128)S(1)} %get-tuple-element.18), channel_id=1, source_target_pairs={{0,1},{1,2},{2,3},{3,4},{4,5},{5,6},{6,7},{7,8},{8,9},{9,10},{10,1... | collective-permute-start | bytes 3145736 | tf_op jit(solution)/shard_map/ppermute | solution.py:304
  57.5 66.6 %collective-permute-start.7 = (f32[2,4,2,2,64,128]{5,4,3,2,1,0:T(8,128)S(1)}, f32[2,4,2,2,64,128]{5,4,3,2,1,0:T(8,128)S(1)}, u32[]{:S(2)}, u32[]{:S(2)}) collective-permute-start(f32[2,4,2,2,64,128]{5,4,3,2,1,0:T(8,128)S(1)} %get-tuple-element.19), channel_id=1, source_target_pairs={{0,1},{1,2},{2,3},{3,4},{4,5},{5,6},{6,7},{7,8},{8,9},{9,10},{10,1... | collective-permute-start | bytes 3145736 | tf_op jit(solution)/shard_map/ppermute | solution.py:304
  70.0 54.2 %collective-permute-start.9 = (f32[2,4,2,2,64,128]{5,4,3,2,1,0:T(8,128)S(1)}, f32[2,4,2,2,64,128]{5,4,3,2,1,0:T(8,128)S(1)}, u32[]{:S(2)}, u32[]{:S(2)}) collective-permute-start(f32[2,4,2,2,64,128]{5,4,3,2,1,0:T(8,128)S(1)} %collective-permute-done.8), channel_id=1, source_target_pairs={{0,128},{1,129},{2,130},{3,131},{4,132},{5,133},{6,134},{7,135},{8... | collective-permute-start | bytes 3145736 | tf_op jit(solution)/shard_map/ppermute | solution.py:304
  70.0 2.8 %collective-permute-start.10 = (f32[2,64,128]{2,1,0:T(8,128)S(1)}, f32[2,64,128]{2,1,0:T(8,128)S(1)}, u32[]{:S(2)}, u32[]{:S(2)}) collective-permute-start(f32[2,64,128]{2,1,0:T(8,128)S(1)} %get-tuple-element.17), channel_id=1, source_target_pairs={{0,128},{1,129},{2,130},{3,131},{4,132},{5,133},{6,134},{7,135},{8... | collective-permute-start | bytes 196616 | tf_op jit(solution)/shard_map/ppermute | solution.py:304
  72.7 9.9 %collective-permute-start.11 = (f32[2,64,128]{2,1,0:T(8,128)S(1)}, f32[2,64,128]{2,1,0:T(8,128)S(1)}, u32[]{:S(2)}, u32[]{:S(2)}) collective-permute-start(f32[2,64,128]{2,1,0:T(8,128)S(1)} %add.24), channel_id=1, source_target_pairs={{0,1},{1,0},{2,3},{3,2},{4,5},{5,4},{6,7},{7,6},{8,9},{9,8},{10,11... | collective-permute-start | bytes 196616 | tf_op jit(solution)/shard_map/ppermute | solution.py:344
  82.6 4.6 %collective-permute-start.12 = (f32[2,64,128]{2,1,0:T(8,128)S(1)}, f32[2,64,128]{2,1,0:T(8,128)S(1)}, u32[]{:S(2)}, u32[]{:S(2)}) collective-permute-start(f32[2,64,128]{2,1,0:T(8,128)S(1)} %add.25), channel_id=1, source_target_pairs={{0,3},{1,2},{2,1},{3,0},{4,7},{5,6},{6,5},{7,4},{8,11},{9,10},{10,... | collective-permute-start | bytes 196616 | tf_op jit(solution)/shard_map/ppermute | solution.py:344
  87.3 4.9 %collective-permute-start.13 = (f32[2,64,128]{2,1,0:T(8,128)S(1)}, f32[2,64,128]{2,1,0:T(8,128)S(1)}, u32[]{:S(2)}, u32[]{:S(2)}) collective-permute-start(f32[2,64,128]{2,1,0:T(8,128)S(1)} %add.26), channel_id=1, source_target_pairs={{0,4},{1,5},{2,6},{3,7},{4,0},{5,1},{6,2},{7,3},{8,12},{9,13},{10,... | collective-permute-start | bytes 196616 | tf_op jit(solution)/shard_map/ppermute | solution.py:344
  92.2 6.9 %collective-permute-start.14 = (f32[2,64,128]{2,1,0:T(8,128)S(1)}, f32[2,64,128]{2,1,0:T(8,128)S(1)}, u32[]{:S(2)}, u32[]{:S(2)}) collective-permute-start(f32[2,64,128]{2,1,0:T(8,128)S(1)} %add.27), channel_id=1, source_target_pairs={{0,12},{1,13},{2,14},{3,15},{4,8},{5,9},{6,10},{7,11},{8,4},{9,5},... | collective-permute-start | bytes 196616 | tf_op jit(solution)/shard_map/ppermute | solution.py:344
  99.1 7.8 %collective-permute-start.15 = (f32[2,64,128]{2,1,0:T(8,128)S(1)}, f32[2,64,128]{2,1,0:T(8,128)S(1)}, u32[]{:S(2)}, u32[]{:S(2)}) collective-permute-start(f32[2,64,128]{2,1,0:T(8,128)S(1)} %add.28), channel_id=1, source_target_pairs={{0,16},{1,17},{2,18},{3,19},{4,20},{5,21},{6,22},{7,23},{8,24},{9,... | collective-permute-start | bytes 196616 | tf_op jit(solution)/shard_map/ppermute | solution.py:344
  106.9 5.4 %collective-permute-start.16 = (f32[2,64,128]{2,1,0:T(8,128)S(1)}, f32[2,64,128]{2,1,0:T(8,128)S(1)}, u32[]{:S(2)}, u32[]{:S(2)}) collective-permute-start(f32[2,64,128]{2,1,0:T(8,128)S(1)} %add.29), channel_id=1, source_target_pairs={{0,32},{1,33},{2,34},{3,35},{4,36},{5,37},{6,38},{7,39},{8,40},{9,... | collective-permute-start | bytes 196616 | tf_op jit(solution)/shard_map/ppermute | solution.py:344
  112.4 10.1 %collective-permute-start.17 = (f32[2,64,128]{2,1,0:T(8,128)S(1)}, f32[2,64,128]{2,1,0:T(8,128)S(1)}, u32[]{:S(2)}, u32[]{:S(2)}) collective-permute-start(f32[2,64,128]{2,1,0:T(8,128)S(1)} %add.30), channel_id=1, source_target_pairs={{0,112},{1,113},{2,114},{3,115},{4,116},{5,117},{6,118},{7,119},{8... | collective-permute-start | bytes 196616 | tf_op jit(solution)/shard_map/ppermute | solution.py:344
  119.5 4.6 %collective-permute-start.1 = (s32[8]{0:T(128)S(1)}, s32[8]{0:T(128)S(1)}, u32[]{:S(2)}, u32[]{:S(2)}) collective-permute-start(s32[8]{0:T(128)S(1)} %collective-permute-done.cols_ref.swap_cols), channel_id=1, source_target_pairs={{0,128},{1,129},{2,130},{3,131},{4,132},{5,133},{6,134},{7,135},{8... | collective-permute-start | bytes 104 | tf_op jit(solution)/shard_map/ppermute | solution.py:304

commit v2 on v1

--- a/solution.py
+++ b/solution.py
@@ -61,25 +61,23 @@
             out_ref[item, part, first + s] = turned[:, :size]
 
 
-def cut_halo_kernel(cols_ref, mine_ref, theirs_ref, pass_ref, keep_ref):
+def cut_kernel(across, cols_ref, mine_ref, theirs_ref, out_ref):
     depth = lax.axis_index("depth")
     group = mine_ref.shape[1]
 
-    @pl.loop(0, keep_ref.shape[0])
+    @pl.loop(0, out_ref.shape[0])
     def _(item):
-        for out_ref, slot in ((pass_ref, 2 * item + 1 - depth), (keep_ref, 2 * item + depth)):
-            cut_piece(mine_ref, out_ref, item, cols_ref[slot], depth * group)
-            cut_piece(theirs_ref, out_ref, item, cols_ref[slot], (1 - depth) * group)
-
-
-def cut_own_kernel(cols_ref, mine_ref, theirs_ref, own_ref):
+        slot = 2 * item + (1 - depth if across else depth)
+        cut_piece(mine_ref, out_ref, item, cols_ref[slot], depth * group)
+        cut_piece(theirs_ref, out_ref, item, cols_ref[slot], (1 - depth) * group)
+
+
+def cut_mine_kernel(cols_ref, mine_ref, own_ref):
     depth = lax.axis_index("depth")
-    group = mine_ref.shape[1]
 
     @pl.loop(0, own_ref.shape[0])
     def _(item):
-        cut_piece(mine_ref, own_ref, item, cols_ref[2 * item + depth], depth * group)
-        cut_piece(theirs_ref, own_ref, item, cols_ref[2 * item + depth], (1 - depth) * group)
+        cut_piece(mine_ref, own_ref, item, cols_ref[2 * item + depth], 0)
 
 
 def split3(x):
@@ -110,7 +108,8 @@
 def compute_kernel(
     counts_ref,
     rows_ref,
-    own,
+    own_mine,
+    own_theirs,
     halo_keep,
     halo_swap,
     probe_ref,
@@ -132,8 +131,8 @@
 ):
     depth, tile = lax.axis_index("depth"), lax.axis_index("tile")
     filled = counts_ref[tile]
-    items, parts, slices, strip, size = own.shape
-    per = slices // 2
+    items, parts, per, strip, size = own_mine.shape
+    slices = 2 * per
     pairs = range(items // 2)
     half = size // 2
     mine, theirs = depth * per, (1 - depth) * per
@@ -151,8 +150,10 @@
         for part in range(parts):
             for s in range(slices):
                 stack[s, pl.ds(from_keep, half), :] = halo_keep[item, part, s]
-                stack[s, half : half + strip, :] = own[item, part, s]
                 stack[s, pl.ds(from_swap, half), :] = halo_swap[item, part, s]
+            for s in range(per):
+                stack[mine + s, half : half + strip, :] = own_mine[item, part, s]
+                stack[theirs + s, half : half + strip, :] = own_theirs[item, part, s]
             for s in range(slices):
                 trans[p, s, part * size : (part + 1) * size, q * size : (q + 1) * size] = stack[
                     s, pl.ds(offset, size), :
@@ -306,23 +307,29 @@
     swap_cols = send(scan_cols, asks)
     theirs = send(transmission, swaps)
     bank = jax.ShapeDtypeStruct((items, parts, slices, strip, size), F32)
-    cut_pass, cut_keep = call(
-        cut_halo_kernel, [SMEM, VMEM, VMEM], [bank] * 2, (swap_cols, transmission, theirs)
-    )
-    passed = send(cut_pass, moves)
-    halo_keep = send(cut_keep, moves)
+    piece = jax.ShapeDtypeStruct((items, parts, per, strip, size), F32)
+    own_mine = call(cut_mine_kernel, [SMEM, VMEM], piece, (scan_cols, transmission))
+    halos = []
+    for across in (True, False):
+        cut = call(
+            functools.partial(cut_kernel, across),
+            [SMEM, VMEM, VMEM],
+            bank,
+            (swap_cols, transmission, theirs),
+        )
+        halos.append(send(cut, moves))
+    passed, halo_keep = halos
     halo_swap = send(passed, swaps)
     keep_cols = send(swap_cols, swaps)
-    own = call(cut_own_kernel, [SMEM, VMEM, VMEM], bank, (scan_cols, transmission, theirs))
-
-    piece = jax.ShapeDtypeStruct((items, parts, per, strip, size), F32)
+    own_theirs = call(cut_mine_kernel, [SMEM, VMEM], piece, (scan_cols, theirs))
+
     both = jax.ShapeDtypeStruct((n_depth, items, parts, per, half, size), F32)
     crossing = jax.ShapeDtypeStruct((3, items, parts, per, half, size), F32)
     results = call(
         compute_kernel,
-        [SMEM, SMEM] + [VMEM] * 7,
+        [SMEM, SMEM] + [VMEM] * 8,
         [piece, both, both, crossing] + [jax.ShapeDtypeStruct((parts, half, size), F32)] * 2,
-        (tile_counts, scan_rows, own, halo_keep, halo_swap, probe, diffraction)
+        (tile_counts, scan_rows, own_mine, own_theirs, halo_keep, halo_swap, probe, diffraction)
         + tuple(jnp.asarray(v) for v in tables(size)),
         scratch=[
             pltpu.VMEM((slices, 2 * half + strip, size), F32),

time: 128 us -> 128 us (level)
  waiting for transfers between devices: 57 us -> 54.8 us
  Pallas kernels: 18.9 us -> 20.6 us
    ppermute x11, waiting for transfers between devices: 32.8 us -> 30.6 us  [send(): return lax.ppermute(value, AXES, pairs)]
    pallas_call x5 -> x7, Pallas kernels: 18.9 us -> 20.6 us  [call(): pl.pallas_call(kernel, out_shape=out_shapes if single else tuple(out_shap...]
  transfers between devices with their start and end apart: 18 -> 18, of which waited for: 13 -> 13; matrix products, arithmetic and copies ran while one was open for 1% -> 1% of each run, Pallas kernels for 2% -> 4%
where the time goes in v2:
time: 128 us; the launch traced here: 127 us
  waiting for transfers between devices  54.8 us (43%)
  starting transfers between devices  47.8 us (37%)
  Pallas kernels  20.6 us (16%)
  local copies, waits for them, and re-layouts  1.72 us (1%)
    ppermute x11, waiting for transfers between devices, send(): return lax.ppermute(value, AXES, pairs)  30.6 us
    ppermute x7, starting transfers between devices, work(): total = total + lax.ppermute(total, AXES, pairs)  25.4 us
    ppermute x7, waiting for transfers between devices, work(): total = total + lax.ppermute(total, AXES, pairs)  24.2 us
    ppermute x11, starting transfers between devices, send(): return lax.ppermute(value, AXES, pairs)  22.3 us
    pallas_call x7, Pallas kernels, call(): pl.pallas_call(kernel, out_shape=out_shapes if single else tuple(out_shap...  20.6 us
  transfers between devices with their start and end apart: 18, of which 13 were waited for; matrix products, arithmetic and copies ran while one was open for 1% of the time, Pallas kernels for 4%

profile of v2, /device:TPU:2, one launch (start us, length us, event | category | flops | bytes accessed | tf_op | source)
XLA Modules:
  0.0 126.5 jit_solution(17026011644928414066)
XLA Ops:
  0.6 0.1 collective-permute-start.2
  0.7 4.2 %collective-permute-start = (s32[8]{0:T(128)}, s32[8]{0:T(128)S(1)}, u32[]{:S(2)}, u32[]{:S(2)}) collective-permute-start(s32[8]{0:T(128)} %own_cols.1), channel_id=1, source_target_pairs={{1,0},{2,1},{3,2},{4,3},{5,4},{6,5},{7,6},{8,7},{9,8},{10,9},{11,1... | collective-permute-start | bytes 104 | tf_op jit(solution)/shard_map/ppermute | solution.py:305
  4.9 1.4 %collective-permute-done.cols_ref.swap_cols = s32[8]{0:T(128)S(1)} collective-permute-done((s32[8]{0:T(128)}, s32[8]{0:T(128)S(1)}, u32[]{:S(2)}, u32[]{:S(2)}) %collective-permute-start) | collective-permute-done | bytes 64 | tf_op jit(solution)/shard_map/ppermute | solution.py:305
  6.3 1.6 %copy-done = f32[2,2,64,2048]{3,2,1,0:T(8,128)S(1)} copy-done((f32[2,2,64,2048]{3,2,1,0:T(8,128)S(1)}, f32[2,2,64,2048]{3,2,1,0:T(8,128)}, u32[]{:S(2)}) %copy-start) | copy-done | bytes 2097176
  7.9 1.4 %shard_map.98 = f32[4,2,4,64,128]{4,3,2,1,0:T(8,128)S(1)} custom-call(s32[8]{0:T(128)S(1)} %collective-permute-done.cols_ref.swap_cols, f32[2,2,64,2048]{3,2,1,0:T(8,128)S(1)} %copy-done, f32[2,2,64,2048]{3,2,1,0:T(8,128)S(1)} %collective-permute-done.2.mine_ref.theirs_ref), custom_call_target="tpu_custom_call" | custom-call | flops 1048576 | bytes 1048576 | tf_op jit(solution)/shard_map/pallas_call | solution.py:279
  9.3 0.0 copy-start.1
  9.4 0.0 copy-start.2
  9.4 3.5 %collective-permute-start.4 = (f32[4,2,4,64,128]{4,3,2,1,0:T(8,128)S(1)}, f32[4,2,4,64,128]{4,3,2,1,0:T(8,128)S(1)}, u32[]{:S(2)}, u32[]{:S(2)}) collective-permute-start(f32[4,2,4,64,128]{4,3,2,1,0:T(8,128)S(1)} %shard_map.98), channel_id=1, source_target_pairs={{0,1},{1,2},{2,3},{3,4},{4,5},{5,6},{6,7},{7,8},{8,9},{9,10},{10,1... | collective-permute-start | bytes 3145736 | tf_op jit(solution)/shard_map/ppermute | solution.py:305
  12.9 1.4 %shard_map.97 = f32[4,2,4,64,128]{4,3,2,1,0:T(8,128)S(1)} custom-call(s32[8]{0:T(128)S(1)} %collective-permute-done.cols_ref.swap_cols, f32[2,2,64,2048]{3,2,1,0:T(8,128)S(1)} %copy-done, f32[2,2,64,2048]{3,2,1,0:T(8,128)S(1)} %collective-permute-done.2.mine_ref.theirs_ref), custom_call_target="tpu_custom_call" | custom-call | flops 1048576 | bytes 1048576 | tf_op jit(solution)/shard_map/pallas_call | solution.py:279
  14.3 0.0 copy-start.3
  14.3 0.0 copy-start.4
  14.3 0.0 copy-start.5
  14.4 0.0 copy-start.6
  14.4 0.0 copy-start.7
  14.4 0.0 copy-start.8
  14.4 5.3 %collective-permute-start.3 = (f32[4,2,4,64,128]{4,3,2,1,0:T(8,128)S(1)}, f32[4,2,4,64,128]{4,3,2,1,0:T(8,128)S(1)}, u32[]{:S(2)}, u32[]{:S(2)}) collective-permute-start(f32[4,2,4,64,128]{4,3,2,1,0:T(8,128)S(1)} %shard_map.97), channel_id=1, source_target_pairs={{0,1},{1,2},{2,3},{3,4},{4,5},{5,6},{6,7},{7,8},{8,9},{9,10},{10,1... | collective-permute-start | bytes 3145736 | tf_op jit(solution)/shard_map/ppermute | solution.py:305
  19.7 6.4 %collective-permute-done.4 = f32[4,2,4,64,128]{4,3,2,1,0:T(8,128)S(1)} collective-permute-done((f32[4,2,4,64,128]{4,3,2,1,0:T(8,128)S(1)}, f32[4,2,4,64,128]{4,3,2,1,0:T(8,128)S(1)}, u32[]{:S(2)}, u32[]{:S(2)}) %collective-permute-start.4) | collective-permute-done | bytes 1048608 | tf_op jit(solution)/shard_map/ppermute | solution.py:305
  26.2 1.1 shard_map.95.own_mine
  27.3 1.1 shard_map.96.own_theirs
  28.5 9.0 %collective-permute-done.3.halo_keep = f32[4,2,4,64,128]{4,3,2,1,0:T(8,128)S(1)} collective-permute-done((f32[4,2,4,64,128]{4,3,2,1,0:T(8,128)S(1)}, f32[4,2,4,64,128]{4,3,2,1,0:T(8,128)S(1)}, u32[]{:S(2)}, u32[]{:S(2)}) %collective-permute-start.3) | collective-permute-done | bytes 1048608 | tf_op jit(solution)/shard_map/ppermute | solution.py:305
  37.4 0.0 collective-permute-done.5.halo_swap
  37.5 11.8 %shard_map.99 = (f32[4,2,2,64,128]{4,3,2,1,0:T(8,128)S(1)}, f32[2,4,2,2,64,128]{5,4,3,2,1,0:T(8,128)S(1)}, f32[2,4,2,2,64,128]{5,4,3,2,1,0:T(8,128)S(1)}, f32[3,...) custom-call(s32[128]{0:T(128)S(1)} %copy-done.3, s32[8]{0:T(128)S(1)} %copy-done.6, ...), custom_call_target="tpu_custom_call" | custom-call | flops 6442450944 | bytes 8388608 | tf_op jit(solution)/shard_map/pallas_call | solution.py:279
  49.3 0.1 collective-permute-start.6
  49.4 3.4 %collective-permute-done.6.crossed = f32[3,4,2,2,64,128]{5,4,3,2,1,0:T(8,128)S(1)} collective-permute-done((f32[3,4,2,2,64,128]{5,4,3,2,1,0:T(8,128)S(1)}, f32[3,4,2,2,64,128]{5,4,3,2,1,0:T(8,128)S(1)}, u32[]{:S(2)}, u32[]{:S(2)}) %collective-permute-start.6) | collective-permute-done | bytes 1572896 | tf_op jit(solution)/shard_map/ppermute | solution.py:305
  52.8 0.1 slice_dynamic-update-slice_fusion
  52.9 4.2 %collective-permute-start.8 = (f32[2,4,2,2,64,128]{5,4,3,2,1,0:T(8,128)S(1)}, f32[2,4,2,2,64,128]{5,4,3,2,1,0:T(8,128)S(1)}, u32[]{:S(2)}, u32[]{:S(2)}) collective-permute-start(f32[2,4,2,2,64,128]{5,4,3,2,1,0:T(8,128)S(1)} %get-tuple-element.14), channel_id=1, source_target_pairs={{0,1},{1,2},{2,3},{3,4},{4,5},{5,6},{6,7},{7,8},{8,9},{9,10},{10,1... | collective-permute-start | bytes 3145736 | tf_op jit(solution)/shard_map/ppermute | solution.py:305
  57.1 4.4 %collective-permute-start.7 = (f32[2,4,2,2,64,128]{5,4,3,2,1,0:T(8,128)S(1)}, f32[2,4,2,2,64,128]{5,4,3,2,1,0:T(8,128)S(1)}, u32[]{:S(2)}, u32[]{:S(2)}) collective-permute-start(f32[2,4,2,2,64,128]{5,4,3,2,1,0:T(8,128)S(1)} %get-tuple-element.15), channel_id=1, source_target_pairs={{0,1},{1,2},{2,3},{3,4},{4,5},{5,6},{6,7},{7,8},{8,9},{9,10},{10,1... | collective-permute-start | bytes 3145736 | tf_op jit(solution)/shard_map/ppermute | solution.py:305
  61.5 8.1 %collective-permute-done.8 = f32[2,4,2,2,64,128]{5,4,3,2,1,0:T(8,128)S(1)} collective-permute-done((f32[2,4,2,2,64,128]{5,4,3,2,1,0:T(8,128)S(1)}, f32[2,4,2,2,64,128]{5,4,3,2,1,0:T(8,128)S(1)}, u32[]{:S(2)}, u32[]{:S(2)}) %collective-permute-start.8) | collective-permute-done | bytes 1048608 | tf_op jit(solution)/shard_map/ppermute | solution.py:305
  69.6 0.0 collective-permute-start.9
  69.6 0.5 collective-permute-start.10
  70.1 2.2 %collective-permute-done.10 = f32[2,64,128]{2,1,0:T(8,128)S(1)} collective-permute-done((f32[2,64,128]{2,1,0:T(8,128)S(1)}, f32[2,64,128]{2,1,0:T(8,128)S(1)}, u32[]{:S(2)}, u32[]{:S(2)}) %collective-permute-start.10) | collective-permute-done | bytes 65568 | tf_op jit(solution)/shard_map/ppermute | solution.py:305
  72.3 0.1 collective-permute-start.11
  72.4 9.8 %collective-permute-done.11 = f32[2,64,128]{2,1,0:T(8,128)S(1)} collective-permute-done((f32[2,64,128]{2,1,0:T(8,128)S(1)}, f32[2,64,128]{2,1,0:T(8,128)S(1)}, u32[]{:S(2)}, u32[]{:S(2)}) %collective-permute-start.11) | collective-permute-done | bytes 65568 | tf_op jit(solution)/shard_map/ppermute | solution.py:351
  82.2 2.4 %collective-permute-start.12 = (f32[2,64,128]{2,1,0:T(8,128)S(1)}, f32[2,64,128]{2,1,0:T(8,128)S(1)}, u32[]{:S(2)}, u32[]{:S(2)}) collective-permute-start(f32[2,64,128]{2,1,0:T(8,128)S(1)} %add.25), channel_id=1, source_target_pairs={{0,3},{1,2},{2,1},{3,0},{4,7},{5,6},{6,5},{7,4},{8,11},{9,10},{10,... | collective-permute-start | bytes 196616 | tf_op jit(solution)/shard_map/ppermute | solution.py:351
  84.6 2.2 %collective-permute-done.12 = f32[2,64,128]{2,1,0:T(8,128)S(1)} collective-permute-done((f32[2,64,128]{2,1,0:T(8,128)S(1)}, f32[2,64,128]{2,1,0:T(8,128)S(1)}, u32[]{:S(2)}, u32[]{:S(2)}) %collective-permute-start.12) | collective-permute-done | bytes 65568 | tf_op jit(solution)/shard_map/ppermute | solution.py:351
  86.9 2.6 %collective-permute-start.13 = (f32[2,64,128]{2,1,0:T(8,128)S(1)}, f32[2,64,128]{2,1,0:T(8,128)S(1)}, u32[]{:S(2)}, u32[]{:S(2)}) collective-permute-start(f32[2,64,128]{2,1,0:T(8,128)S(1)} %add.26), channel_id=1, source_target_pairs={{0,4},{1,5},{2,6},{3,7},{4,0},{5,1},{6,2},{7,3},{8,12},{9,13},{10,... | collective-permute-start | bytes 196616 | tf_op jit(solution)/shard_map/ppermute | solution.py:351
  89.5 2.2 %collective-permute-done.13 = f32[2,64,128]{2,1,0:T(8,128)S(1)} collective-permute-done((f32[2,64,128]{2,1,0:T(8,128)S(1)}, f32[2,64,128]{2,1,0:T(8,128)S(1)}, u32[]{:S(2)}, u32[]{:S(2)}) %collective-permute-start.13) | collective-permute-done | bytes 65568 | tf_op jit(solution)/shard_map/ppermute | solution.py:351
  91.8 4.7 %collective-permute-start.14 = (f32[2,64,128]{2,1,0:T(8,128)S(1)}, f32[2,64,128]{2,1,0:T(8,128)S(1)}, u32[]{:S(2)}, u32[]{:S(2)}) collective-permute-start(f32[2,64,128]{2,1,0:T(8,128)S(1)} %add.27), channel_id=1, source_target_pairs={{0,12},{1,13},{2,14},{3,15},{4,8},{5,9},{6,10},{7,11},{8,4},{9,5},... | collective-permute-start | bytes 196616 | tf_op jit(solution)/shard_map/ppermute | solution.py:351
  96.5 2.2 %collective-permute-done.14 = f32[2,64,128]{2,1,0:T(8,128)S(1)} collective-permute-done((f32[2,64,128]{2,1,0:T(8,128)S(1)}, f32[2,64,128]{2,1,0:T(8,128)S(1)}, u32[]{:S(2)}, u32[]{:S(2)}) %collective-permute-start.14) | collective-permute-done | bytes 65568 | tf_op jit(solution)/shard_map/ppermute | solution.py:351
  98.7 5.3 %collective-permute-start.15 = (f32[2,64,128]{2,1,0:T(8,128)S(1)}, f32[2,64,128]{2,1,0:T(8,128)S(1)}, u32[]{:S(2)}, u32[]{:S(2)}) collective-permute-start(f32[2,64,128]{2,1,0:T(8,128)S(1)} %add.28), channel_id=1, source_target_pairs={{0,16},{1,17},{2,18},{3,19},{4,20},{5,21},{6,22},{7,23},{8,24},{9,... | collective-permute-start | bytes 196616 | tf_op jit(solution)/shard_map/ppermute | solution.py:351
  104.0 2.5 %collective-permute-done.15 = f32[2,64,128]{2,1,0:T(8,128)S(1)} collective-permute-done((f32[2,64,128]{2,1,0:T(8,128)S(1)}, f32[2,64,128]{2,1,0:T(8,128)S(1)}, u32[]{:S(2)}, u32[]{:S(2)}) %collective-permute-start.15) | collective-permute-done | bytes 65568 | tf_op jit(solution)/shard_map/ppermute | solution.py:351
  106.5 3.2 %collective-permute-start.16 = (f32[2,64,128]{2,1,0:T(8,128)S(1)}, f32[2,64,128]{2,1,0:T(8,128)S(1)}, u32[]{:S(2)}, u32[]{:S(2)}) collective-permute-start(f32[2,64,128]{2,1,0:T(8,128)S(1)} %add.29), channel_id=1, source_target_pairs={{0,32},{1,33},{2,34},{3,35},{4,36},{5,37},{6,38},{7,39},{8,40},{9,... | collective-permute-start | bytes 196616 | tf_op jit(solution)/shard_map/ppermute | solution.py:351
  109.7 2.2 %collective-permute-done.16 = f32[2,64,128]{2,1,0:T(8,128)S(1)} collective-permute-done((f32[2,64,128]{2,1,0:T(8,128)S(1)}, f32[2,64,128]{2,1,0:T(8,128)S(1)}, u32[]{:S(2)}, u32[]{:S(2)}) %collective-permute-start.16) | collective-permute-done | bytes 65568 | tf_op jit(solution)/shard_map/ppermute | solution.py:351
  112.0 7.1 %collective-permute-start.17 = (f32[2,64,128]{2,1,0:T(8,128)S(1)}, f32[2,64,128]{2,1,0:T(8,128)S(1)}, u32[]{:S(2)}, u32[]{:S(2)}) collective-permute-start(f32[2,64,128]{2,1,0:T(8,128)S(1)} %add.30), channel_id=1, source_target_pairs={{0,112},{1,113},{2,114},{3,115},{4,116},{5,117},{6,118},{7,119},{8... | collective-permute-start | bytes 196616 | tf_op jit(solution)/shard_map/ppermute | solution.py:351
  119.1 2.9 %collective-permute-done.17 = f32[2,64,128]{2,1,0:T(8,128)S(1)} collective-permute-done((f32[2,64,128]{2,1,0:T(8,128)S(1)}, f32[2,64,128]{2,1,0:T(8,128)S(1)}, u32[]{:S(2)}, u32[]{:S(2)}) %collective-permute-start.17) | collective-permute-done | bytes 65568 | tf_op jit(solution)/shard_map/ppermute | solution.py:351
  122.1 0.6 add.31
  122.7 1.0 shard_map.100.so_far
  123.7 2.8 %shard_map.101 = f32[2,2,64,2048]{3,2,1,0:T(8,128)} custom-call(s32[128]{0:T(128)S(1)} %copy-done.3, s32[8]{0:T(128)S(1)} %collective-permute-done.1.keep_cols, s32[8]{0:T(128)S(1)} %collective-permute-done.cols_ref.swap_cols, f32[2,4,2,2,64,128]{5,4,3,2,1,0:T(8,128)S(1)} %collective-permute-done.7.keep, ...), custom_call_target="tpu_custom_call" | custom-call | flops 1048576 | bytes 1048576 | tf_op jit(solution)/shard_map/pallas_call | solution.py:279
  (22 shorter events, 0.1 us)
Async XLA Ops:
  0.6 5.7 %collective-permute-start.2 = (f32[2,2,64,2048]{3,2,1,0:T(8,128)}, f32[2,2,64,2048]{3,2,1,0:T(8,128)S(1)}, u32[]{:S(2)}, u32[]{:S(2)}) collective-permute-start(f32[2,2,64,2048]{3,2,1,0:T(8,128)} %mine_ref.5), channel_id=1, source_target_pairs={{0,128},{1,129},{2,130},{3,131},{4,132},{5,133},{6,134},{7,135},{8... | collective-permute-start | bytes 6291464 | tf_op jit(solution)/shard_map/ppermute | solution.py:305
  0.7 5.6 %collective-permute-start = (s32[8]{0:T(128)}, s32[8]{0:T(128)S(1)}, u32[]{:S(2)}, u32[]{:S(2)}) collective-permute-start(s32[8]{0:T(128)} %own_cols.1), channel_id=1, source_target_pairs={{1,0},{2,1},{3,2},{4,3},{5,4},{6,5},{7,6},{8,7},{9,8},{10,9},{11,1... | collective-permute-start | bytes 104 | tf_op jit(solution)/shard_map/ppermute | solution.py:305
  6.3 1.6 %copy-start = (f32[2,2,64,2048]{3,2,1,0:T(8,128)S(1)}, f32[2,2,64,2048]{3,2,1,0:T(8,128)}, u32[]{:S(2)}) copy-start(f32[2,2,64,2048]{3,2,1,0:T(8,128)} %mine_ref.5) | copy-start | bytes 6291460
  9.3 16.9 %copy-start.1 = (f32[2,2,64,2048]{3,2,1,0:T(8,128)S(1)}, f32[2,2,64,2048]{3,2,1,0:T(8,128)}, u32[]{:S(2)}) copy-start(f32[2,2,64,2048]{3,2,1,0:T(8,128)} %mine_ref.5) | copy-start | bytes 6291460
  9.4 16.8 %copy-start.2 = (s32[8]{0:T(128)S(1)}, s32[8]{0:T(128)}, u32[]{:S(2)}) copy-start(s32[8]{0:T(128)} %own_cols.1) | copy-start | bytes 100
  9.4 16.8 %collective-permute-start.4 = (f32[4,2,4,64,128]{4,3,2,1,0:T(8,128)S(1)}, f32[4,2,4,64,128]{4,3,2,1,0:T(8,128)S(1)}, u32[]{:S(2)}, u32[]{:S(2)}) collective-permute-start(f32[4,2,4,64,128]{4,3,2,1,0:T(8,128)S(1)} %shard_map.98), channel_id=1, source_target_pairs={{0,1},{1,2},{2,3},{3,4},{4,5},{5,6},{6,7},{7,8},{8,9},{9,10},{10,1... | collective-permute-start | bytes 3145736 | tf_op jit(solution)/shard_map/ppermute | solution.py:305
  14.3 23.1 %copy-start.3 = (s32[128]{0:T(128)S(1)}, s32[128]{0:T(128)}, u32[]{:S(2)}) copy-start(s32[128]{0:T(128)} %counts_ref.5) | copy-start | bytes 1540
  14.3 23.1 %copy-start.4 = (f32[8,128,128]{2,1,0:T(8,128)S(1)}, f32[8,128,128]{2,1,0:T(8,128)}, u32[]{:S(2)}) copy-start(f32[8,128,128]{2,1,0:T(8,128)} %diff_ref.1) | copy-start | bytes 1572868
  14.3 23.1 %copy-start.5 = (f32[2,128,128]{2,1,0:T(8,128)S(1)}, f32[2,128,128]{2,1,0:T(8,128)}, u32[]{:S(2)}) copy-start(f32[2,128,128]{2,1,0:T(8,128)} %probe_ref.1) | copy-start | bytes 393220
  14.4 23.1 %copy-start.6 = (s32[8]{0:T(128)S(1)}, s32[8]{0:T(128)}, u32[]{:S(2)}) copy-start(s32[8]{0:T(128)} %rows_ref.1) | copy-start | bytes 100
  14.4 23.1 %copy-start.7 = (bf16[4,256,256]{2,1,0:T(8,128)(2,1)S(1)}, bf16[4,256,256]{2,1,0:T(8,128)(2,1)}, u32[]{:S(2)}) copy-start(bf16[4,256,256]{2,1,0:T(8,128)(2,1)} %constant.8.clone.dft_ref) | copy-start | bytes 1572868
  14.4 23.1 %copy-start.8 = (f32[2,128,128]{2,1,0:T(8,128)S(1)}, f32[2,128,128]{2,1,0:T(8,128)}, u32[]{:S(2)}) copy-start(f32[2,128,128]{2,1,0:T(8,128)} %constant.9.clone.kern_ref) | copy-start | bytes 393220
  14.4 23.0 %collective-permute-start.3 = (f32[4,2,4,64,128]{4,3,2,1,0:T(8,128)S(1)}, f32[4,2,4,64,128]{4,3,2,1,0:T(8,128)S(1)}, u32[]{:S(2)}, u32[]{:S(2)}) collective-permute-start(f32[4,2,4,64,128]{4,3,2,1,0:T(8,128)S(1)} %shard_map.97), channel_id=1, source_target_pairs={{0,1},{1,2},{2,3},{3,4},{4,5},{5,6},{6,7},{7,8},{8,9},{9,10},{10,1... | collective-permute-start | bytes 3145736 | tf_op jit(solution)/shard_map/ppermute | solution.py:305
  26.2 11.2 %collective-permute-start.5 = (f32[4,2,4,64,128]{4,3,2,1,0:T(8,128)S(1)}, f32[4,2,4,64,128]{4,3,2,1,0:T(8,128)S(1)}, u32[]{:S(2)}, u32[]{:S(2)}) collective-permute-start(f32[4,2,4,64,128]{4,3,2,1,0:T(8,128)S(1)} %collective-permute-done.4), channel_id=1, source_target_pairs={{0,128},{1,129},{2,130},{3,131},{4,132},{5,133},{6,134},{7,135},{8... | collective-permute-start | bytes 3145736 | tf_op jit(solution)/shard_map/ppermute | solution.py:305
  49.3 3.5 %collective-permute-start.6 = (f32[3,4,2,2,64,128]{5,4,3,2,1,0:T(8,128)S(1)}, f32[3,4,2,2,64,128]{5,4,3,2,1,0:T(8,128)S(1)}, u32[]{:S(2)}, u32[]{:S(2)}) collective-permute-start(f32[3,4,2,2,64,128]{5,4,3,2,1,0:T(8,128)S(1)} %get-tuple-element.9), channel_id=1, source_target_pairs={{0,128},{1,129},{2,130},{3,131},{4,132},{5,133},{6,134},{7,135},{8... | collective-permute-start | bytes 4718600 | tf_op jit(solution)/shard_map/ppermute | solution.py:305
  52.9 16.7 %collective-permute-start.8 = (f32[2,4,2,2,64,128]{5,4,3,2,1,0:T(8,128)S(1)}, f32[2,4,2,2,64,128]{5,4,3,2,1,0:T(8,128)S(1)}, u32[]{:S(2)}, u32[]{:S(2)}) collective-permute-start(f32[2,4,2,2,64,128]{5,4,3,2,1,0:T(8,128)S(1)} %get-tuple-element.14), channel_id=1, source_target_pairs={{0,1},{1,2},{2,3},{3,4},{4,5},{5,6},{6,7},{7,8},{8,9},{9,10},{10,1... | collective-permute-start | bytes 3145736 | tf_op jit(solution)/shard_map/ppermute | solution.py:305
  57.1 66.6 %collective-permute-start.7 = (f32[2,4,2,2,64,128]{5,4,3,2,1,0:T(8,128)S(1)}, f32[2,4,2,2,64,128]{5,4,3,2,1,0:T(8,128)S(1)}, u32[]{:S(2)}, u32[]{:S(2)}) collective-permute-start(f32[2,4,2,2,64,128]{5,4,3,2,1,0:T(8,128)S(1)} %get-tuple-element.15), channel_id=1, source_target_pairs={{0,1},{1,2},{2,3},{3,4},{4,5},{5,6},{6,7},{7,8},{8,9},{9,10},{10,1... | collective-permute-start | bytes 3145736 | tf_op jit(solution)/shard_map/ppermute | solution.py:305
  69.6 54.2 %collective-permute-start.9 = (f32[2,4,2,2,64,128]{5,4,3,2,1,0:T(8,128)S(1)}, f32[2,4,2,2,64,128]{5,4,3,2,1,0:T(8,128)S(1)}, u32[]{:S(2)}, u32[]{:S(2)}) collective-permute-start(f32[2,4,2,2,64,128]{5,4,3,2,1,0:T(8,128)S(1)} %collective-permute-done.8), channel_id=1, source_target_pairs={{0,128},{1,129},{2,130},{3,131},{4,132},{5,133},{6,134},{7,135},{8... | collective-permute-start | bytes 3145736 | tf_op jit(solution)/shard_map/ppermute | solution.py:305
  69.6 2.8 %collective-permute-start.10 = (f32[2,64,128]{2,1,0:T(8,128)S(1)}, f32[2,64,128]{2,1,0:T(8,128)S(1)}, u32[]{:S(2)}, u32[]{:S(2)}) collective-permute-start(f32[2,64,128]{2,1,0:T(8,128)S(1)} %get-tuple-element.13), channel_id=1, source_target_pairs={{0,128},{1,129},{2,130},{3,131},{4,132},{5,133},{6,134},{7,135},{8... | collective-permute-start | bytes 196616 | tf_op jit(solution)/shard_map/ppermute | solution.py:305
  72.3 9.9 %collective-permute-start.11 = (f32[2,64,128]{2,1,0:T(8,128)S(1)}, f32[2,64,128]{2,1,0:T(8,128)S(1)}, u32[]{:S(2)}, u32[]{:S(2)}) collective-permute-start(f32[2,64,128]{2,1,0:T(8,128)S(1)} %add.24), channel_id=1, source_target_pairs={{0,1},{1,0},{2,3},{3,2},{4,5},{5,4},{6,7},{7,6},{8,9},{9,8},{10,11... | collective-permute-start | bytes 196616 | tf_op jit(solution)/shard_map/ppermute | solution.py:351
  82.2 4.6 %collective-permute-start.12 = (f32[2,64,128]{2,1,0:T(8,128)S(1)}, f32[2,64,128]{2,1,0:T(8,128)S(1)}, u32[]{:S(2)}, u32[]{:S(2)}) collective-permute-start(f32[2,64,128]{2,1,0:T(8,128)S(1)} %add.25), channel_id=1, source_target_pairs={{0,3},{1,2},{2,1},{3,0},{4,7},{5,6},{6,5},{7,4},{8,11},{9,10},{10,... | collective-permute-start | bytes 196616 | tf_op jit(solution)/shard_map/ppermute | solution.py:351
  86.9 4.9 %collective-permute-start.13 = (f32[2,64,128]{2,1,0:T(8,128)S(1)}, f32[2,64,128]{2,1,0:T(8,128)S(1)}, u32[]{:S(2)}, u32[]{:S(2)}) collective-permute-start(f32[2,64,128]{2,1,0:T(8,128)S(1)} %add.26), channel_id=1, source_target_pairs={{0,4},{1,5},{2,6},{3,7},{4,0},{5,1},{6,2},{7,3},{8,12},{9,13},{10,... | collective-permute-start | bytes 196616 | tf_op jit(solution)/shard_map/ppermute | solution.py:351
  91.8 6.9 %collective-permute-start.14 = (f32[2,64,128]{2,1,0:T(8,128)S(1)}, f32[2,64,128]{2,1,0:T(8,128)S(1)}, u32[]{:S(2)}, u32[]{:S(2)}) collective-permute-start(f32[2,64,128]{2,1,0:T(8,128)S(1)} %add.27), channel_id=1, source_target_pairs={{0,12},{1,13},{2,14},{3,15},{4,8},{5,9},{6,10},{7,11},{8,4},{9,5},... | collective-permute-start | bytes 196616 | tf_op jit(solution)/shard_map/ppermute | solution.py:351
  98.7 7.8 %collective-permute-start.15 = (f32[2,64,128]{2,1,0:T(8,128)S(1)}, f32[2,64,128]{2,1,0:T(8,128)S(1)}, u32[]{:S(2)}, u32[]{:S(2)}) collective-permute-start(f32[2,64,128]{2,1,0:T(8,128)S(1)} %add.28), channel_id=1, source_target_pairs={{0,16},{1,17},{2,18},{3,19},{4,20},{5,21},{6,22},{7,23},{8,24},{9,... | collective-permute-start | bytes 196616 | tf_op jit(solution)/shard_map/ppermute | solution.py:351
  106.5 5.4 %collective-permute-start.16 = (f32[2,64,128]{2,1,0:T(8,128)S(1)}, f32[2,64,128]{2,1,0:T(8,128)S(1)}, u32[]{:S(2)}, u32[]{:S(2)}) collective-permute-start(f32[2,64,128]{2,1,0:T(8,128)S(1)} %add.29), channel_id=1, source_target_pairs={{0,32},{1,33},{2,34},{3,35},{4,36},{5,37},{6,38},{7,39},{8,40},{9,... | collective-permute-start | bytes 196616 | tf_op jit(solution)/shard_map/ppermute | solution.py:351
  112.0 10.1 %collective-permute-start.17 = (f32[2,64,128]{2,1,0:T(8,128)S(1)}, f32[2,64,128]{2,1,0:T(8,128)S(1)}, u32[]{:S(2)}, u32[]{:S(2)}) collective-permute-start(f32[2,64,128]{2,1,0:T(8,128)S(1)} %add.30), channel_id=1, source_target_pairs={{0,112},{1,113},{2,114},{3,115},{4,116},{5,117},{6,118},{7,119},{8... | collective-permute-start | bytes 196616 | tf_op jit(solution)/shard_map/ppermute | solution.py:351
  119.1 4.6 %collective-permute-start.1 = (s32[8]{0:T(128)S(1)}, s32[8]{0:T(128)S(1)}, u32[]{:S(2)}, u32[]{:S(2)}) collective-permute-start(s32[8]{0:T(128)S(1)} %collective-permute-done.cols_ref.swap_cols), channel_id=1, source_target_pairs={{0,128},{1,129},{2,130},{3,131},{4,132},{5,133},{6,134},{7,135},{8... | collective-permute-start | bytes 104 | tf_op jit(solution)/shard_map/ppermute | solution.py:305
